TPU v7x, 256 devices: a whole 4x4x8 slice. The times are simulated.
256 devices in a mesh: cfg: 2 (over core), img: 4 (over x), seq: 32 (over z, y).
Axes of the slice: x: 4, y: 4, z: 8, core: 2. Of those that a mesh axis runs over, the one named last changes fastest.
Arguments:
- img_qkv: bfloat16 [2, 4, 4096, 3, 2048], P('cfg', 'img', 'seq'), may hold values from -5 to 5
- txt_kv: bfloat16 [2, 4, 256, 2, 2048], P('cfg', 'img', 'seq'), may hold values from -5 to 5
- readout: bfloat16 [2048, 64], replicated, may hold values from -0.125 to 0.125
- old_velocity: float32 [4, 4096, 64], P('img', 'seq'), may hold values from -6 to 6
- noise: float32 [4, 4096, 64], P('img', 'seq'), may hold values from -5 to 5
- step_ratio: float32 [4], P('img'), may hold values from 0.2 to 0.8
- rewards: float32 [4], P('img'), may hold values from -6 to 6
- guidance: float32 [], replicated, may hold values from 1.5 to 3
Outputs:
- img_grad: bfloat16 [2, 4, 4096, 3, 2048], P('cfg', 'img', 'seq')
- txt_grad: bfloat16 [2, 4, 256, 2, 2048], P('cfg', 'img', 'seq')
- readout_grad: float32 [2048, 64], replicated
- ratio: float32 [4], P('img')
All inputs are finite; a program needn't handle non-finite values.
Results may differ from a plain program's by a relative error of at most 0.009.
Values may be sent and summed in bfloat16 or wider, within the bound.
A program may use at most 128 MiB of HBM per device.

v0:
```python
import jax
import jax.numpy as jnp
from jax import lax
from jax.sharding import Mesh
from jax.sharding import PartitionSpec as P

HEADS = 16
HEAD_DIM = 128
SEQ = ("seq_0", "seq_1")


def from_everyone(value, axis):
    copies = jnp.broadcast_to(value, (lax.axis_size(axis), *value.shape))
    return lax.all_to_all(copies, axis, split_axis=0, concat_axis=0, tiled=True)


def taken_together(value, axis):
    everything = from_everyone(value, axis)
    return jnp.sum(everything, axis=0)


def in_one(arrays, axis):
    line, at, outs = (jnp.concatenate([a.reshape(-1) for a in arrays]), 0, [])
    total = taken_together(line, axis)
    for a in arrays:
        outs.append(total[at : at + a.size].reshape(a.shape))
        at += a.size
    return tuple(outs)


def side_by_side(arrays, axis, split_dim, concat_dim, along):
    ends, at = ([], 0)
    for a in arrays[:-1]:
        at += a.shape[along]
        ends.append(at)
    both = jnp.concatenate(arrays, axis=along)
    return tuple(
        jnp.split(
            lax.all_to_all(both, axis, split_axis=split_dim, concat_axis=concat_dim, tiled=True),
            ends,
            axis=along,
        )
    )


def swapped(block, axis, apart):
    count = lax.axis_size(axis)
    route = []
    for low in range(count):
        high = low | 1 << apart
        if high != low and high < count:
            route += [(low, high), (high, low)]
    return lax.ppermute(block, axis, route)


def split_up(value, dim, count):
    before, after = (value.shape[:dim], value.shape[dim + 1 :])
    return jnp.moveaxis(value.reshape(*before, count, -1, *after), dim, 0)


def sum_at_owner(value, axis, dim):
    blocks = split_up(value, dim, lax.axis_size(axis))
    arrived = lax.all_to_all(blocks, axis, split_axis=0, concat_axis=0, tiled=True)
    return arrived.sum(axis=0)


def sum_by_axis(value, axes, dim):
    far, near = axes
    blocks = split_up(value, dim, lax.axis_size(far))
    nearer = sum_at_owner(blocks, near, dim + 1)
    arrived = lax.all_to_all(nearer, far, split_axis=0, concat_axis=0, tiled=True)
    return arrived.sum(axis=0)


def filled_up(lines, count):
    spare = -len(lines) % count
    return jnp.pad(lines, [(0, spare)] + [(0, 0)] * (lines.ndim - 1))


def laid_out(blocks, dim):
    blocks = jnp.moveaxis(blocks, 0, dim)
    dims = blocks.shape
    return blocks.reshape(*dims[:dim], dims[dim] * dims[dim + 1], *dims[dim + 2 :])


def gather_axes(value, axes, dim):
    far, near = axes
    blocks = from_everyone(from_everyone(value, far), near)
    return laid_out(blocks.swapaxes(0, 1).reshape(-1, *value.shape), dim)


def total_of(value, axes):
    lines = value.reshape(-1, value.shape[-1])
    own = sum_by_axis(filled_up(lines, lax.axis_size(axes[0]) * lax.axis_size(axes[1])), axes, 0)
    whole = gather_axes(own, axes, 0)
    return whole[: len(lines)].reshape(value.shape)


def to_items(rows_whole, copies, groups, width):
    count = rows_whole.shape[0]
    split = rows_whole.reshape(copies, count // copies, groups, width)
    return split.transpose(2, 0, 1, 3).reshape(groups * copies, count // copies, width)


def from_items(items, copies, groups):
    sub_rows = items.shape[1]
    width = items.shape[2]
    split = items.reshape(groups, copies, sub_rows, width)
    return split.transpose(1, 2, 0, 3).reshape(copies * sub_rows, groups * width)


def block_count(total):
    count = max(1, total // 512)
    while total % count:
        count -= 1
    return count


def heads_view(x):
    return x.reshape(x.shape[0], x.shape[1] // HEAD_DIM, HEAD_DIM)


def attend_forward(queries, keys, values):
    blocks = block_count(queries.shape[0])
    scale = HEAD_DIM ** (-0.5)
    key_heads = heads_view(keys)
    value_heads = heads_view(values)
    query_blocks = heads_view(queries).reshape(blocks, -1, key_heads.shape[1], HEAD_DIM)

    def one_block(block):
        scores = (
            jnp.einsum("qhd,khd->hqk", block, key_heads, preferred_element_type=jnp.float32) * scale
        )
        top = jnp.max(scores, axis=-1, keepdims=True)
        raised = jnp.exp(scores - top)
        probs = (raised / jnp.sum(raised, axis=-1, keepdims=True)).astype(jnp.bfloat16)
        mixed = jnp.einsum("hqk,khd->qhd", probs, value_heads, preferred_element_type=jnp.float32)
        return (probs, mixed.astype(jnp.bfloat16))

    probs, mixed = lax.map(one_block, query_blocks)
    return (probs, mixed.reshape(queries.shape[0], queries.shape[1]))


def attend_backward(queries, keys, values, probs, grad_out):
    blocks = probs.shape[0]
    scale = HEAD_DIM ** (-0.5)
    key_heads = heads_view(keys)
    value_heads = heads_view(values)
    count = key_heads.shape[1]
    query_blocks = heads_view(queries).reshape(blocks, -1, count, HEAD_DIM)
    grad_blocks = heads_view(grad_out).reshape(blocks, -1, count, HEAD_DIM)

    def one_block(carry, inputs):
        block, grad_block, prob = inputs
        grad_probs = jnp.einsum(
            "qhd,khd->hqk", grad_block, value_heads, preferred_element_type=jnp.float32
        )
        weights = prob.astype(jnp.float32)
        delta = jnp.sum(weights * grad_probs, axis=-1, keepdims=True)
        grad_scores = (weights * (grad_probs - delta) * scale).astype(jnp.bfloat16)
        grad_query = jnp.einsum(
            "hqk,khd->qhd", grad_scores, key_heads, preferred_element_type=jnp.float32
        )
        grad_keys = carry[0] + jnp.einsum(
            "hqk,qhd->khd", grad_scores, block, preferred_element_type=jnp.float32
        )
        grad_values = carry[1] + jnp.einsum(
            "hqk,qhd->khd", prob, grad_block, preferred_element_type=jnp.float32
        )
        return ((grad_keys, grad_values), grad_query.astype(jnp.bfloat16))

    zeros = jnp.zeros(key_heads.shape, jnp.float32)
    totals, grad_query = lax.scan(one_block, (zeros, zeros), (query_blocks, grad_blocks, probs))
    return (
        grad_query.reshape(queries.shape),
        totals[0].reshape(keys.shape),
        totals[1].reshape(keys.shape),
    )


def surrogate_gain(ratio, advantage):
    clipped = jnp.clip(ratio, 0.8, 1.2)
    keep = ratio * advantage <= clipped * advantage
    return jnp.where(keep, -ratio * advantage, jnp.zeros_like(ratio))


def on_device(img_qkv, txt_kv, readout, old_velocity, noise, step_ratio, rewards, guidance):
    parts = lax.axis_size(SEQ)
    copies = max(1, parts // HEADS)
    groups = parts // copies
    width = readout.shape[0] // groups
    own = img_qkv[0, 0]
    text = txt_kv[0, 0]
    img_rows = own.shape[0]
    txt_rows = text.shape[0]
    keys = jnp.concatenate([text[:, 0], own[:, 1]], axis=0)
    values = jnp.concatenate([text[:, 1], own[:, 2]], axis=0)
    reward = rewards[0]
    reward_sums = in_one((reward, reward * reward), "img")
    images = lax.axis_size("img")
    mean = reward_sums[0] / images
    spread = jnp.sqrt(jnp.maximum(reward_sums[1] / images - mean * mean, 0.0))
    advantage = (reward - mean) / jnp.maximum(spread, 1.0)
    query_items = to_items(own[:, 0], copies, groups, width)
    key_items = to_items(keys, copies, groups, width)
    value_items = to_items(values, copies, groups, width)
    arrived = (
        lax.all_to_all(query_items, SEQ, split_axis=0, concat_axis=1, tiled=True),
        *side_by_side((key_items, value_items), SEQ, 0, 1, 2),
    )
    queries = arrived[0][0]
    head_keys = arrived[1][0]
    head_values = arrived[2][0]
    other = swapped((head_keys, head_values), SEQ, 0)
    head_keys = jnp.concatenate([head_keys, other[0]], axis=0)
    head_values = jnp.concatenate([head_values, other[1]], axis=0)
    probs, mixed = attend_forward(queries, head_keys, head_values)
    returned = lax.all_to_all(
        mixed.reshape(parts, -1, width), SEQ, split_axis=0, concat_axis=0, tiled=True
    )
    attended = from_items(returned, copies, groups)
    velocity = jnp.dot(attended, readout, preferred_element_type=jnp.float32)
    branch = lax.axis_index("cfg")
    rate = step_ratio[0]
    count = img_rows * parts * velocity.shape[1]
    partner = swapped(velocity, "cfg", 0)
    conditional = jnp.where(branch == 0, velocity, partner)
    unconditional = jnp.where(branch == 0, partner, velocity)
    guided = unconditional + guidance * (conditional - unconditional)
    deviation = rate * (guided - old_velocity[0])
    partial_sum = jnp.sum(noise[0] * deviation - 0.5 * deviation * deviation)
    log_ratio = taken_together(partial_sum, SEQ) / count
    ratio = jnp.exp(log_ratio)
    gain = surrogate_gain(ratio, advantage)
    grad_guided = gain * rate * (noise[0] - deviation)
    grad_velocity = jnp.where(branch == 0, guidance, 1.0 - guidance) * grad_guided
    readout_part = jnp.dot(
        attended.astype(jnp.float32).T, grad_velocity, precision=lax.Precision.HIGHEST
    )
    readout_grad = total_of(readout_part, (("cfg", "img", "seq_0"), "seq_1"))
    grad_attended = jnp.dot(
        grad_velocity, readout.astype(jnp.float32).T, precision=lax.Precision.HIGHEST
    ).astype(jnp.bfloat16)
    grad_items = to_items(grad_attended, copies, groups, width)
    grad_out = lax.all_to_all(grad_items, SEQ, split_axis=0, concat_axis=1, tiled=True)[0]
    grad_query, grad_keys, grad_values = attend_backward(
        queries, head_keys, head_values, probs, grad_out
    )
    middle = grad_keys.shape[0] // 2
    other_grads = (
        swapped(grad_keys[middle:].astype(jnp.bfloat16), SEQ, 0).astype(jnp.float32),
        swapped(grad_values[middle:].astype(jnp.bfloat16), SEQ, 0).astype(jnp.float32),
    )
    grad_keys = grad_keys[:middle] + other_grads[0]
    grad_values = grad_values[:middle] + other_grads[1]
    home = side_by_side(
        (
            grad_query.reshape(parts, -1, width),
            grad_keys.astype(jnp.bfloat16).reshape(parts, -1, width),
            grad_values.astype(jnp.bfloat16).reshape(parts, -1, width),
        ),
        SEQ,
        0,
        0,
        1,
    )
    query_grad = from_items(home[0], copies, groups)
    key_grad = from_items(home[1], copies, groups)
    value_grad = from_items(home[2], copies, groups)
    img_grad = jnp.stack([query_grad, key_grad[txt_rows:], value_grad[txt_rows:]], axis=1)[
        None, None
    ]
    txt_grad = jnp.stack([key_grad[:txt_rows], value_grad[:txt_rows]], axis=1)[None, None]
    return (img_grad, txt_grad, readout_grad, ratio.reshape(1))


def solution(mesh):
    finer = Mesh(
        mesh.devices.reshape(mesh.shape["cfg"], mesh.shape["img"], 8, 4),
        ("cfg", "img", "seq_0", "seq_1"),
    )
    placed = (
        P("cfg", "img", SEQ, None, None),
        P("cfg", "img", SEQ, None, None),
        P(),
        P("img", SEQ, None),
        P("img", SEQ, None),
        P("img"),
        P("img"),
        P(),
    )
    return jax.shard_map(
        on_device,
        mesh=finer,
        in_specs=placed,
        out_specs=(
            P("cfg", "img", SEQ, None, None),
            P("cfg", "img", SEQ, None, None),
            P(),
            P("img"),
        ),
        check_vma=False,
    )
```

profile of v0, /device:TPU:5, one launch (start us, length us, event | category | flops | bytes accessed | tf_op | source)
XLA Modules:
  0.0 412.0 jit_solution(5158069511907869778)
XLA Ops:
  3.0 42.2 %all_to_all.72 = bf16[32,68,256]{2,1,0:T(8,128)(2,1)S(1)} all-to-all(bf16[32,68,256]{2,1,0:T(8,128)(2,1)S(1)} %pad_maximum_fusion.1), channel_id=1, replica_groups=mesh['cfg'=2,'img'=4,'seq_0'=8,'seq_1'=4] {'seq_0','seq_1'}, dimensions={0} | all-to-all | bytes 2228224 | tf_op jit(solution)/shard_map/all_to_all | solution.py:39
  47.6 5.6 %all-to-all-start = ((bf16[32,64,128]{2,1,0:T(8,128)(2,1)}), bf16[32,64,128]{2,1,0:T(8,128)(2,1)S(1)}, u32[]{:S(2)}, u32[]{:S(2)}) async-start(bf16[32,64,128]{2,1,0:T(8,128)(2,1)} %bitcast.10), calls=%async_computation | async-start | bytes 1048576 | tf_op jit(solution)/shard_map/all_to_all | solution.py:208
  59.5 15.9 %collective-permute-done.1 = bf16[2176,128]{1,0:T(8,128)(2,1)S(1)} collective-permute-done((bf16[2176,128]{1,0:T(8,128)(2,1)}, bf16[2176,128]{1,0:T(8,128)(2,1)S(1)}, u32[]{:S(2)}, u32[]{:S(2)}) %collective-permute-start.1) | collective-permute-done | bytes 557088 | tf_op jit(solution)/shard_map/ppermute | solution.py:53
  81.5 32.6 %while.27 = (s32[]{:T(128)}, bf16[4,1,512,4352]{3,2,1,0:T(8,128)(2,1)}, bf16[4,512,1,128]{3,1,2,0:T(8,128)(2,1)S(1)}, bf16[4,512,1,128]{3,1,2,0:T(8,128)(2,1)S(1...) while((s32[]{:T(128)}, bf16[4,1,512,4352]{3,2,1,0:T(8,128)(2,1)}, ...), condition=%wide.region_3.0_spmd, body=%wide.region_0.3_spmd.sunk | while | flops 1160969216 | bytes 42609236 | solution.py:140
  114.8 6.7 %all-to-all-start.2 = ((bf16[32,64,128]{2,1,0:T(8,128)(2,1)}), bf16[32,64,128]{2,1,0:T(8,128)(2,1)S(1)}, u32[]{:S(2)}, u32[]{:S(2)}) async-start(bf16[32,64,128]{2,1,0:T(8,128)(2,1)} %bitcast.284), calls=%async_computation.2 | async-start | bytes 1048576 | tf_op jit(solution)/shard_map/all_to_all | solution.py:218
  122.9 13.5 %all-to-all-done.2 = bf16[32,64,128]{2,1,0:T(8,128)(2,1)S(1)} async-done(((bf16[32,64,128]{2,1,0:T(8,128)(2,1)}), bf16[32,64,128]{2,1,0:T(8,128)(2,1)S(1)}, u32[]{:S(2)}, u32[]{:S(2)}) %all-to-all-start.2) | async-done | bytes 524320 | tf_op jit(solution)/shard_map/all_to_all | solution.py:218
  156.2 6.1 %all-to-all-done.3 = f32[32,1,1]{2,1,0:T(1,128)S(1)} async-done(((f32[32,1,1]{2,1,0:T(1,128)}), f32[32,1,1]{2,1,0:T(1,128)S(1)}, u32[]{:S(2)}, u32[]{:S(2)}) %all-to-all-start.3) | async-done | bytes 160 | tf_op jit(solution)/shard_map/all_to_all | solution.py:14
  166.5 11.7 %all_to_all.73 = f32[4,1,32768]{2,1,0:T(1,128)S(1)} all-to-all(f32[4,1,32768]{2,1,0:T(1,128)} %reshape.207), channel_id=1, replica_groups=mesh['cfg'=2,'img'=4,'seq_0'=8,'seq_1'=4] {'seq_1'}, dimensions={0} | all-to-all | bytes 1048576 | tf_op jit(solution)/shard_map/all_to_all | solution.py:63
  185.2 15.8 %all_to_all.74 = f32[64,1,512]{2,1,0:T(1,128)S(1)} all-to-all(f32[64,1,512]{2,1,0:T(1,128)S(1)} %reshape.209), channel_id=1, replica_groups=mesh['cfg'=2,'img'=4,'seq_0'=8,'seq_1'=4] {'cfg','img','seq_0'}, dimensions={0} | all-to-all | bytes 262144 | tf_op jit(solution)/shard_map/all_to_all | solution.py:71
  203.0 7.7 %all-to-all-start.9 = ((f32[64,1,512]{2,1,0:T(1,128)}), f32[64,1,512]{2,1,0:T(1,128)S(1)}, u32[]{:S(2)}, u32[]{:S(2)}) async-start(f32[64,1,512]{2,1,0:T(1,128)} %reshape.211), calls=%async_computation.9 | async-start | bytes 262144 | tf_op jit(solution)/shard_map/all_to_all | solution.py:14
  212.4 6.8 %all-to-all-done.9 = f32[64,1,512]{2,1,0:T(1,128)S(1)} async-done(((f32[64,1,512]{2,1,0:T(1,128)}), f32[64,1,512]{2,1,0:T(1,128)S(1)}, u32[]{:S(2)}, u32[]{:S(2)}) %all-to-all-start.9) | async-done | bytes 131104 | tf_op jit(solution)/shard_map/all_to_all | solution.py:14
  228.0 11.8 %all-to-all-done.5 = bf16[32,64,128]{2,1,0:T(8,128)(2,1)S(1)} async-done(((bf16[32,64,128]{2,1,0:T(8,128)(2,1)}), bf16[32,64,128]{2,1,0:T(8,128)(2,1)S(1)}, u32[]{:S(2)}, u32[]{:S(2)}) %all-to-all-start.5) | async-done | bytes 524320 | tf_op jit(solution)/shard_map/all_to_all | solution.py:245
  245.0 89.4 %while.28 = (s32[]{:T(128)}, f32[4352,1,128]{0,2,1:T(8,128)S(1)}, f32[4352,1,128]{0,2,1:T(8,128)}, bf16[4,512,1,128]{3,1,2,0:T(8,128)(2,1)}, bf16[4,512,1,128]{3...) while((s32[]{:T(128)}, f32[4352,1,128]{0,2,1:T(8,128)S(1)}, ...), condition=%wide.region_9.10_spmd.clone, body=%wide.region_7.9_spmd.clone.sunk | while | flops 2301820416 | bytes 82713832 | solution.py:173
  249.8 6.6 %fusion.81 = bf16[512,4352]{1,0:T(8,128)(2,1)} fusion(f32[512,4352]{1,0:T(8,128)S(1)} %get-tuple-element.369, f32[512]{0:T(512)S(1)} %get-tuple-element.370, bf16[4,1,512,4352]{3,2,1,0:T(8,128)(2,1)} %get-tuple-element.419, s32[]{:T(128)} %get-tuple-element.403), kind=kLoop, calls=%fused_computation.18.clone.1 | loop fusion | flops 11141120 | bytes 17827844 | tf_op jit(solution)/shard_map/while/body/eval_jaxpr/convert_element_type | solution.py:160
  271.6 6.6 %fusion.81 = bf16[512,4352]{1,0:T(8,128)(2,1)} fusion(f32[512,4352]{1,0:T(8,128)S(1)} %get-tuple-element.369, f32[512]{0:T(512)S(1)} %get-tuple-element.370, bf16[4,1,512,4352]{3,2,1,0:T(8,128)(2,1)} %get-tuple-element.419, s32[]{:T(128)} %get-tuple-element.403), kind=kLoop, calls=%fused_computation.18.clone.1 | loop fusion | flops 11141120 | bytes 17827844 | tf_op jit(solution)/shard_map/while/body/eval_jaxpr/convert_element_type | solution.py:160
  284.2 5.1 %fusion.83 = f32[4352,1,128]{0,2,1:T(8,128)} fusion(bf16[4,1,512,4352]{3,2,1,0:T(8,128)(2,1)} %get-tuple-element.419, s32[]{:T(128)} %get-tuple-element.403, f32[4352,1,128]{0,2,1:T(8,128)} %get-tuple-element.405, pred[]{:T(512)S(6)} %compare.3, bf16[4,512,1,128]{3,1,2,0:T(8,128)(2,1)S(1)} %copy-done.8), kind=kOutput, calls=%fused_computation.22.clone.1 | convolution fusion | flops 571539456 | bytes 9044993 | tf_op jit(solution)/shard_map/while/body/eval_jaxpr/hqk,qhd->khd/dot_general | solution.py:167
  294.1 6.6 %fusion.81 = bf16[512,4352]{1,0:T(8,128)(2,1)} fusion(f32[512,4352]{1,0:T(8,128)S(1)} %get-tuple-element.369, f32[512]{0:T(512)S(1)} %get-tuple-element.370, bf16[4,1,512,4352]{3,2,1,0:T(8,128)(2,1)} %get-tuple-element.419, s32[]{:T(128)} %get-tuple-element.403), kind=kLoop, calls=%fused_computation.18.clone.1 | loop fusion | flops 11141120 | bytes 17827844 | tf_op jit(solution)/shard_map/while/body/eval_jaxpr/convert_element_type | solution.py:160
  306.7 5.1 %fusion.83 = f32[4352,1,128]{0,2,1:T(8,128)} fusion(bf16[4,1,512,4352]{3,2,1,0:T(8,128)(2,1)} %get-tuple-element.419, s32[]{:T(128)} %get-tuple-element.403, f32[4352,1,128]{0,2,1:T(8,128)} %get-tuple-element.405, pred[]{:T(512)S(6)} %compare.3, bf16[4,512,1,128]{3,1,2,0:T(8,128)(2,1)S(1)} %copy-done.8), kind=kOutput, calls=%fused_computation.22.clone.1 | convolution fusion | flops 571539456 | bytes 9044993 | tf_op jit(solution)/shard_map/while/body/eval_jaxpr/hqk,qhd->khd/dot_general | solution.py:167
  316.7 6.6 %fusion.81 = bf16[512,4352]{1,0:T(8,128)(2,1)} fusion(f32[512,4352]{1,0:T(8,128)S(1)} %get-tuple-element.369, f32[512]{0:T(512)S(1)} %get-tuple-element.370, bf16[4,1,512,4352]{3,2,1,0:T(8,128)(2,1)} %get-tuple-element.419, s32[]{:T(128)} %get-tuple-element.403), kind=kLoop, calls=%fused_computation.18.clone.1 | loop fusion | flops 11141120 | bytes 17827844 | tf_op jit(solution)/shard_map/while/body/eval_jaxpr/convert_element_type | solution.py:160
  329.2 5.1 %fusion.83 = f32[4352,1,128]{0,2,1:T(8,128)} fusion(bf16[4,1,512,4352]{3,2,1,0:T(8,128)(2,1)} %get-tuple-element.419, s32[]{:T(128)} %get-tuple-element.403, f32[4352,1,128]{0,2,1:T(8,128)} %get-tuple-element.405, pred[]{:T(512)S(6)} %compare.3, bf16[4,512,1,128]{3,1,2,0:T(8,128)(2,1)S(1)} %copy-done.8), kind=kOutput, calls=%fused_computation.22.clone.1 | convolution fusion | flops 571539456 | bytes 9044993 | tf_op jit(solution)/shard_map/while/body/eval_jaxpr/hqk,qhd->khd/dot_general | solution.py:167
  337.3 9.1 %collective-permute-done.3 = bf16[2176,128]{0,1:T(8,128)(2,1)S(1)} collective-permute-done((bf16[2176,128]{0,1:T(8,128)(2,1)S(1)}, bf16[2176,128]{0,1:T(8,128)(2,1)S(1)}, u32[]{:S(2)}, u32[]{:S(2)}) %collective-permute-start.3) | collective-permute-done | bytes 557088 | tf_op jit(solution)/shard_map/ppermute | solution.py:53
  346.6 11.8 %collective-permute-done.4 = bf16[2176,128]{0,1:T(8,128)(2,1)S(1)} collective-permute-done((bf16[2176,128]{0,1:T(8,128)(2,1)S(1)}, bf16[2176,128]{0,1:T(8,128)(2,1)S(1)}, u32[]{:S(2)}, u32[]{:S(2)}) %collective-permute-start.4) | collective-permute-done | bytes 557088 | tf_op jit(solution)/shard_map/ppermute | solution.py:53
  362.2 8.2 %all-to-all-start.6 = ((bf16[32,200,128]{2,1,0:T(8,128)(2,1)}), bf16[32,200,128]{2,1,0:T(8,128)(2,1)S(1)}, u32[]{:S(2)}, u32[]{:S(2)}) async-start(bf16[32,200,128]{2,1,0:T(8,128)(2,1)} %pad_maximum_fusion), calls=%async_computation.6 | async-start | bytes 3276800 | tf_op jit(solution)/shard_map/all_to_all | solution.py:39
  377.4 29.8 %all-to-all-done.6 = bf16[32,200,128]{2,1,0:T(8,128)(2,1)S(1)} async-done(((bf16[32,200,128]{2,1,0:T(8,128)(2,1)}), bf16[32,200,128]{2,1,0:T(8,128)(2,1)S(1)}, u32[]{:S(2)}, u32[]{:S(2)}) %all-to-all-start.6) | async-done | bytes 1638432 | tf_op jit(solution)/shard_map/all_to_all | solution.py:39
  (180 shorter events, 159.8 us)
Async XLA Ops:
  0.6 137.9 %copy-start = (bf16[2048,64]{0,1:T(8,128)(2,1)S(1)}, bf16[2048,64]{0,1:T(8,128)(2,1)}, u32[]{:S(2)}) copy-start(bf16[2048,64]{0,1:T(8,128)(2,1)} %param.14) | copy-start | bytes 786436
  46.4 8.7 %copy-start.9 = (bf16[2176,128]{1,0:T(8,128)(2,1)}, bf16[2176,128]{1,0:T(8,128)(2,1)S(1)}, u32[]{:S(2)}) copy-start(bf16[2176,128]{1,0:T(8,128)(2,1)S(1)} %get-tuple-element.260) | copy-start | bytes 1671172
  46.4 12.0 %collective-permute-start = (bf16[2176,128]{1,0:T(8,128)(2,1)S(1)}, bf16[2176,128]{1,0:T(8,128)(2,1)S(1)}, u32[]{:S(2)}, u32[]{:S(2)}) collective-permute-start(bf16[2176,128]{1,0:T(8,128)(2,1)S(1)} %get-tuple-element.260), channel_id=1, source_target_pairs={{0,1},{1,0},{2,3},{3,2},{4,5},{5,4},{6,7},{7,6},{8,9},{9,8},{10,11... | collective-permute-start | bytes 1671176 | tf_op jit(solution)/shard_map/ppermute | solution.py:53
  47.6 29.0 %all-to-all-start = ((bf16[32,64,128]{2,1,0:T(8,128)(2,1)}), bf16[32,64,128]{2,1,0:T(8,128)(2,1)S(1)}, u32[]{:S(2)}, u32[]{:S(2)}) async-start(bf16[32,64,128]{2,1,0:T(8,128)(2,1)} %bitcast.10), calls=%async_computation | async-start | bytes 1048576 | tf_op jit(solution)/shard_map/all_to_all | solution.py:208
  53.9 21.6 %collective-permute-start.1 = (bf16[2176,128]{1,0:T(8,128)(2,1)}, bf16[2176,128]{1,0:T(8,128)(2,1)S(1)}, u32[]{:S(2)}, u32[]{:S(2)}) collective-permute-start(bf16[2176,128]{1,0:T(8,128)(2,1)} %get-tuple-element.259), channel_id=1, source_target_pairs={{0,1},{1,0},{2,3},{3,2},{4,5},{5,4},{6,7},{7,6},{8,9},{9,8},{10,11... | collective-permute-start | bytes 1671176 | tf_op jit(solution)/shard_map/ppermute | solution.py:53
  77.1 36.9 %all-to-all-start.4 = ((f32[4,1,2]{2,1,0:T(1,128)}), f32[4,1,2]{2,1,0:T(1,128)S(1)}, u32[]{:S(2)}, u32[]{:S(2)}) async-start(f32[4,1,2]{2,1,0:T(1,128)} %broadcast_in_dim.41), calls=%async_computation.4 | async-start | bytes 4096 | tf_op jit(solution)/shard_map/all_to_all | solution.py:14
  114.0 42.1 %copy-start.6 = (bf16[4,512,1,128]{3,1,2,0:T(8,128)(2,1)}, bf16[4,512,1,128]{3,1,2,0:T(8,128)(2,1)S(1)}, u32[]{:S(2)}) copy-start(bf16[4,512,1,128]{3,1,2,0:T(8,128)(2,1)S(1)} %get-tuple-element.429) | copy-start | bytes 1572868
  114.0 69.2 %copy-start.3 = (bf16[4352,1,128]{2,0,1:T(8,128)(2,1)}, bf16[4352,1,128]{2,0,1:T(8,128)(2,1)S(1)}, u32[]{:S(2)}) copy-start(bf16[4352,1,128]{2,0,1:T(8,128)(2,1)S(1)} %get-tuple-element.425) | copy-start | bytes 3342340
  114.0 69.2 %copy-start.5 = (bf16[4352,1,128]{2,0,1:T(8,128)(2,1)}, bf16[4352,1,128]{2,0,1:T(8,128)(2,1)S(1)}, u32[]{:S(2)}) copy-start(bf16[4352,1,128]{2,0,1:T(8,128)(2,1)S(1)} %get-tuple-element.426) | copy-start | bytes 3342340
  114.8 21.5 %all-to-all-start.2 = ((bf16[32,64,128]{2,1,0:T(8,128)(2,1)}), bf16[32,64,128]{2,1,0:T(8,128)(2,1)S(1)}, u32[]{:S(2)}, u32[]{:S(2)}) async-start(bf16[32,64,128]{2,1,0:T(8,128)(2,1)} %bitcast.284), calls=%async_computation.2 | async-start | bytes 1048576 | tf_op jit(solution)/shard_map/all_to_all | solution.py:218
  138.8 7.3 %collective-permute-start.2 = (f32[128,64]{0,1:T(8,128)S(1)}, f32[128,64]{0,1:T(8,128)S(1)}, u32[]{:S(2)}, u32[]{:S(2)}) collective-permute-start(f32[128,64]{0,1:T(8,128)S(1)} %fusion.35), channel_id=1, source_target_pairs={{0,128},{128,0},{1,129},{129,1},{2,130},{130,2},{3,131},{131,3},{4... | collective-permute-start | bytes 98312 | tf_op jit(solution)/shard_map/ppermute | solution.py:53
  149.4 12.9 %all-to-all-start.3 = ((f32[32,1,1]{2,1,0:T(1,128)}), f32[32,1,1]{2,1,0:T(1,128)S(1)}, u32[]{:S(2)}, u32[]{:S(2)}) async-start(f32[32,1,1]{2,1,0:T(1,128)} %broadcast_in_dim.40), calls=%async_computation.3 | async-start | bytes 32768 | tf_op jit(solution)/shard_map/all_to_all | solution.py:14
  184.1 26.6 %copy-start.13 = (f32[1,128,64]{1,2,0:T(8,128)S(1)}, f32[1,128,64]{1,2,0:T(8,128)}, u32[]{:S(2)}) copy-start(f32[1,128,64]{1,2,0:T(8,128)} %param.16) | copy-start | bytes 98308
  184.1 26.6 %copy-start.14 = (f32[128,64]{0,1:T(8,128)S(1)}, f32[128,64]{0,1:T(8,128)}, u32[]{:S(2)}) copy-start(f32[128,64]{0,1:T(8,128)} %get-tuple-element.249) | copy-start | bytes 98308
  203.0 16.3 %all-to-all-start.9 = ((f32[64,1,512]{2,1,0:T(1,128)}), f32[64,1,512]{2,1,0:T(1,128)S(1)}, u32[]{:S(2)}, u32[]{:S(2)}) async-start(f32[64,1,512]{2,1,0:T(1,128)} %reshape.211), calls=%async_computation.9 | async-start | bytes 262144 | tf_op jit(solution)/shard_map/all_to_all | solution.py:14
  219.3 20.5 %all-to-all-start.5 = ((bf16[32,64,128]{2,1,0:T(8,128)(2,1)}), bf16[32,64,128]{2,1,0:T(8,128)(2,1)S(1)}, u32[]{:S(2)}, u32[]{:S(2)}) async-start(bf16[32,64,128]{2,1,0:T(8,128)(2,1)} %bitcast.35), calls=%async_computation.5 | async-start | bytes 1048576 | tf_op jit(solution)/shard_map/all_to_all | solution.py:245
  239.7 122.5 %all-to-all-start.10 = ((f32[4,1,32768]{2,1,0:T(1,128)}), f32[4,1,32768]{2,1,0:T(1,128)}, u32[]{:S(2)}, u32[]{:S(2)}) async-start(f32[4,1,32768]{2,1,0:T(1,128)} %reshape.213), calls=%async_computation.10 | async-start | bytes 1048576 | tf_op jit(solution)/shard_map/all_to_all | solution.py:14
  256.4 4.0 copy-start.4
  278.2 4.0 copy-start.4
  300.7 4.0 copy-start.4
  323.3 4.0 copy-start.4
  334.4 12.0 %collective-permute-start.3 = (bf16[2176,128]{0,1:T(8,128)(2,1)S(1)}, bf16[2176,128]{0,1:T(8,128)(2,1)S(1)}, u32[]{:S(2)}, u32[]{:S(2)}) collective-permute-start(bf16[2176,128]{0,1:T(8,128)(2,1)S(1)} %fusion.33), channel_id=1, source_target_pairs={{0,1},{1,0},{2,3},{3,2},{4,5},{5,4},{6,7},{7,6},{8,9},{9,8},{10,11... | collective-permute-start | bytes 1671176 | tf_op jit(solution)/shard_map/ppermute | solution.py:53
  337.0 21.4 %collective-permute-start.4 = (bf16[2176,128]{0,1:T(8,128)(2,1)S(1)}, bf16[2176,128]{0,1:T(8,128)(2,1)S(1)}, u32[]{:S(2)}, u32[]{:S(2)}) collective-permute-start(bf16[2176,128]{0,1:T(8,128)(2,1)S(1)} %fusion.34), channel_id=1, source_target_pairs={{0,1},{1,0},{2,3},{3,2},{4,5},{5,4},{6,7},{7,6},{8,9},{9,8},{10,11... | collective-permute-start | bytes 1671176 | tf_op jit(solution)/shard_map/ppermute | solution.py:53
  362.2 45.0 %all-to-all-start.6 = ((bf16[32,200,128]{2,1,0:T(8,128)(2,1)}), bf16[32,200,128]{2,1,0:T(8,128)(2,1)S(1)}, u32[]{:S(2)}, u32[]{:S(2)}) async-start(bf16[32,200,128]{2,1,0:T(8,128)(2,1)} %pad_maximum_fusion), calls=%async_computation.6 | async-start | bytes 3276800 | tf_op jit(solution)/shard_map/all_to_all | solution.py:39
  (17 other events, 32.4 us)
where the time goes:
time: 420 us; the launch traced here: 412 us
  waiting for transfers between devices  108 us (26%)
  matrix products  72.3 us (17%)
  blocking collectives  69.8 us (17%)
  other arithmetic  65.8 us (16%)
  starting transfers between devices  52.2 us (12%)
  local copies, waits for them, and re-layouts  36 us (9%)
  between operations  7.66 us (2%)
    all_to_all x1, blocking collectives, side_by_side(): lax.all_to_all(both, axis, split_axis=split_dim, concat_axis=concat_dim,...  42.2 us
    ppermute x5, waiting for transfers between devices, swapped(): return lax.ppermute(block, axis, route)  40.1 us
    all_to_all x1, waiting for transfers between devices, side_by_side(): lax.all_to_all(both, axis, split_axis=split_dim, concat_axis=concat_dim,...  29.8 us
    convert_element_type x4, other arithmetic, one_block(): grad_scores = (weights * (grad_probs - delta) * scale).astype(jnp.bfloat16)  26.3 us
    all_to_all x4, starting transfers between devices, from_everyone(): return lax.all_to_all(copies, axis, split_axis=0, concat_axis=0, tiled=True)  20.7 us
    dot_general x4, matrix products, one_block(): jnp.einsum('hqk,qhd->khd', prob, grad_block, preferred_element_type=jnp.f...  19.7 us
    dot_general x4, matrix products, one_block(): jnp.einsum('qhd,khd->hqk', grad_block, value_heads, preferred_element_typ...  16.2 us
    all_to_all x1, blocking collectives, sum_by_axis(): lax.all_to_all(nearer, far, split_axis=0, concat_axis=0, tiled=True)  15.8 us
  transfers between devices with their start and end apart: 13, of which 9 were waited for; matrix products, arithmetic and copies ran while one was open for 35% of the time, Pallas kernels for 0%

commit v1 on v0

v1 whole, which is shorter than its diff:
```python
import functools

import jax
import jax.numpy as jnp
from jax import lax
from jax.experimental import pallas as pl
from jax.experimental.pallas import tpu as pltpu
from jax.sharding import PartitionSpec as P

D = 128
C = 64
HALF = 64
TXT = 8
YN = 4
QB = 256
KB = 256
MESH = pl.DeviceIdType.MESH
F32 = jnp.float32
BF16 = jnp.bfloat16
NT = (((1,), (1,)), ((), ()))
TN = (((0,), (0,)), ((), ()))
ANY = pl.BlockSpec(memory_space=pl.ANY)
VMEM = pl.BlockSpec(memory_space=pltpu.VMEM)
SMEM = pl.BlockSpec(memory_space=pltpu.SMEM)
LIMIT = 60 * 1024 * 1024


def iota(shape, dim):
    return lax.broadcasted_iota(jnp.int32, shape, dim)


def put(src, dst, send, recv, core, chip):
    here = jnp.logical_and(core == lax.axis_index("cfg"), chip == lax.axis_index("seq"))

    @pl.when(here)
    def _():
        pltpu.make_async_copy(src, dst, recv).start()

    @pl.when(jnp.logical_not(here))
    def _():
        away(src, dst, send, recv, {"cfg": core, "seq": chip}).start()


def away(src, dst, send, recv, device):
    return pltpu.make_async_remote_copy(
        src_ref=src,
        dst_ref=dst,
        send_sem=send,
        recv_sem=recv,
        device_id=device,
        device_id_type=MESH,
    )


def drain(ref, sem):
    pltpu.make_async_copy(ref, ref, sem).wait()


def signal_plane(chips):
    c, s = lax.axis_index("cfg"), lax.axis_index("seq")
    barrier = pltpu.get_barrier_semaphore()

    def one(k, carry):
        n = lax.rem(c * chips + s + k, 2 * chips)
        pl.semaphore_signal(
            barrier,
            inc=1,
            device_id={"cfg": n // chips, "seq": lax.rem(n, chips)},
            device_id_type=MESH,
        )
        return carry

    lax.fori_loop(1, 2 * chips, one, 0)
    return barrier


def spread_kernel(S, img, tx, rt, kv, qo, txo, vbuf, vrp, txb, vsem, ks, kr, qs, qr, ts, tr, fs, fr, gs, gr):
    H = S // 2
    c, s = lax.axis_index("cfg"), lax.axis_index("seq")
    vcopy = pltpu.make_async_copy(img.at[2], vbuf, vsem)
    vcopy.start()
    barrier = signal_plane(S)
    vcopy.wait()

    def narrow(h, carry):
        cols = pl.ds(pl.multiple_of(h * D, D), D)
        r = rt[:, cols]
        twice = jnp.concatenate([r, r], axis=0)
        x = lax.dot_general(vbuf[:, cols], twice, NT, preferred_element_type=F32)
        low = iota((HALF // 2, D), 1) < C
        for j in range(2):
            first = x[HALF * j : HALF * j + HALF // 2]
            second = x[HALF * j + HALF // 2 : HALF * j + HALF]
            vrp[h, j] = jnp.where(low, first, second).astype(BF16)
        t = tx[:, cols]
        y = lax.dot_general(t, twice, NT, preferred_element_type=F32)
        y = jnp.where(iota(y.shape, 1) < C, y, 0.0)
        txb[h] = jnp.where(iota(y.shape, 0) < TXT, t.astype(F32), y).astype(BF16)
        return carry

    lax.fori_loop(0, H, narrow, 0)
    pl.semaphore_wait(barrier, 2 * S - 1)
    side = s // H

    def send_keys(k, carry):
        h = lax.rem(s // 2 + k, H)
        chip = 2 * h + c
        cols = pl.ds(pl.multiple_of(h * D, D), D)
        for j in range(2):
            put(img.at[1, pl.ds(HALF * j, HALF), cols], kv.at[0, s, pl.ds(0, HALF)], ks.at[h, j], kr.at[s], j, chip)
            put(vrp.at[h, j], kv.at[0, s, pl.ds(HALF, HALF // 2)], ks.at[h, j], kr.at[s], j, chip)
        put(txb.at[h], txo.at[0, lax.rem(s, H)], ts.at[h], tr.at[lax.rem(s, H)], side, chip)
        return carry

    lax.fori_loop(0, H, send_keys, 0)

    def send_queries(k, carry):
        h = lax.rem(s // 2 + k, H)
        chip = 2 * h + c
        cols = pl.ds(pl.multiple_of(h * D, D), D)
        for j in range(2):
            put(img.at[0, pl.ds(HALF * j, HALF), cols], qo.at[s], qs.at[h, j], qr.at[s], j, chip)
        return carry

    lax.fori_loop(0, H, send_queries, 0)

    other = {"cfg": 1 - c}

    def forward(k, carry):
        for odd in range(2):
            src = 2 * lax.rem(s // 2 - k + H, H) + odd
            drain(kv.at[0, src], kr.at[src])
            away(kv.at[0, src], kv.at[1, src], fs.at[src], fr.at[src], other).start()
        return carry

    lax.fori_loop(0, H, forward, 0)

    def forward_text(k, carry):
        drain(txo.at[0, k], tr.at[k])
        away(txo.at[0, k], txo.at[1, k], gs.at[k], gr.at[k], other).start()
        return carry

    lax.fori_loop(0, H, forward_text, 0)

    def finish(k, carry):
        for odd in range(2):
            src = 2 * k + odd
            drain(qo.at[src], qr.at[src])
            drain(kv.at[1, src], fr.at[src])
            drain(kv.at[1, src], fs.at[src])
        drain(txo.at[1, k], gr.at[k])
        drain(txo.at[1, k], gs.at[k])
        chip = 2 * k + c
        for j in range(2):
            @pl.when(jnp.logical_not(jnp.logical_and(chip == s, j == c)))
            def _():
                drain(kv.at[0, 0], ks.at[k, j])
                drain(qo.at[0], qs.at[k, j])

        @pl.when(jnp.logical_not(jnp.logical_and(chip == s, side == c)))
        def _():
            drain(txo.at[0, 0], ts.at[k])

        return carry

    lax.fori_loop(0, H, finish, 0)


def spread(S, img, tx, rt):
    H = S // 2
    dma = pltpu.SemaphoreType.DMA
    return pl.pallas_call(
        functools.partial(spread_kernel, S),
        out_shape=(
            jax.ShapeDtypeStruct((2, S, HALF + HALF // 2, D), BF16),
            jax.ShapeDtypeStruct((S, HALF, D), BF16),
            jax.ShapeDtypeStruct((2, H, 2 * TXT, D), BF16),
        ),
        in_specs=[ANY, VMEM, VMEM],
        out_specs=(ANY, ANY, ANY),
        scratch_shapes=[
            pltpu.VMEM(img.shape[1:], BF16),
            pltpu.VMEM((H, 2, HALF // 2, D), BF16),
            pltpu.VMEM((H, 2 * TXT, D), BF16),
            dma,
            dma((H, 2)),
            dma((S,)),
            dma((H, 2)),
            dma((S,)),
            dma((H,)),
            dma((H,)),
            dma((S,)),
            dma((S,)),
            dma((H,)),
            dma((H,)),
        ],
        compiler_params=pltpu.CompilerParams(collective_id=0, has_side_effects=True),
        name="spread",
    )(img, tx, rt)


def chunks(total):
    return [(at, min(KB, total - at)) for at in range(0, total, KB)]


def pack_pair(x):
    top, low = x[: C // 2], x[C // 2 :]
    lower = iota(top.shape, 1) < HALF
    return (
        jnp.where(lower, top, pltpu.roll(low, HALF, 1)),
        jnp.where(lower, pltpu.roll(top, HALF, 1), low),
    )


def unpack_pair(a, b):
    lower = iota(a.shape, 1) < HALF
    return jnp.concatenate(
        [jnp.where(lower, a, pltpu.roll(b, HALF, 1)), jnp.where(lower, pltpu.roll(a, HALF, 1), b)], axis=0
    )


def forward_kernel(S, guidance, kv, tx, q, e_out, msg, out_t, linv, keys, keys_t, narrow, narrow_t, scores):
    nk = keys.shape[0]
    third = HALF // 2

    @pl.when(pl.program_id(0) == 0)
    def _():
        for p in range(2):
            packed = kv[p, :, HALF:, :].reshape(third * S, D)
            turned = packed.astype(F32).T
            for ab in range(2):
                rows = pl.ds((2 * p + ab) * third * S, third * S)
                part = kv[p, :, third * ab : third * ab + third, :].reshape(third * S, D)
                keys[rows] = part
                keys_t[:, rows] = part.astype(F32).T.astype(BF16)
                one = turned[C * ab : C * ab + C]
                narrow_t[:, rows] = one.astype(BF16)
                narrow[rows] = one.T.astype(BF16)
        text = tx[...].astype(F32)
        tk = text[:, :, :TXT, :].reshape(TXT * S, D)
        tv = text[:, :, TXT:, :].reshape(TXT * S, D)
        rows = pl.ds(2 * HALF * S, TXT * S)
        keys[rows] = tk.astype(BF16)
        keys_t[:, rows] = tk.T.astype(BF16)
        tvt = tv.T[:C]
        narrow_t[:, rows] = tvt.astype(BF16)
        narrow[rows] = tvt.T.astype(BF16)

    q_t = q[...].reshape(QB, D).astype(F32).T.astype(BF16)
    top = jnp.full((8, QB), -jnp.inf, F32)
    for at, size in chunks(nk):
        st = jnp.dot(keys[at : at + size], q_t, preferred_element_type=F32)
        scores[at : at + size] = st
        top = jnp.maximum(top, jnp.max(st.reshape(size // 8, 8, QB), axis=0))
    top = jnp.max(top, axis=0, keepdims=True)
    scale = D ** (-0.5) * 1.4426950408889634
    total = jnp.zeros((8, QB), F32)
    mixed = jnp.zeros((C, QB), F32)
    for at, size in chunks(nk):
        e = jnp.exp2((scores[at : at + size] - top) * scale)
        total = total + jnp.sum(e.reshape(size // 8, 8, QB), axis=0)
        e = e.astype(BF16)
        e_out[0, at : at + size] = e
        mixed = mixed + jnp.dot(narrow_t[:, at : at + size], e, preferred_element_type=F32)
    inverse = 1.0 / jnp.sum(total, axis=0, keepdims=True)
    linv[0] = inverse
    mixed = mixed * inverse
    out_t[0] = mixed
    branch = lax.rem(lax.axis_index("seq"), 2)
    share = jnp.where(branch == 0, guidance[0, 0], 1.0 - guidance[0, 0])
    for m in range(QB // D):
        a, b = pack_pair(mixed[:, D * m : D * m + D] * share)
        msg[2 * m] = a.astype(BF16)
        msg[2 * m + 1] = b.astype(BF16)


def forward(S, guidance, kv, tx, q):
    nk = (2 * HALF + TXT) * S
    nb = S * HALF // QB
    per = QB // HALF
    whole = lambda *shape: pl.BlockSpec(shape, lambda i: (0,) * len(shape))
    block = lambda *shape: pl.BlockSpec(shape, lambda i: (i,) + (0,) * (len(shape) - 1))
    return pl.pallas_call(
        functools.partial(forward_kernel, S),
        grid=(nb,),
        out_shape=(
            jax.ShapeDtypeStruct((nb, nk, QB), BF16),
            jax.ShapeDtypeStruct((S, C // 2, D), BF16),
            jax.ShapeDtypeStruct((nb, C, QB), F32),
            jax.ShapeDtypeStruct((nb, 1, QB), F32),
            jax.ShapeDtypeStruct((nk, D), BF16),
            jax.ShapeDtypeStruct((D, nk), BF16),
            jax.ShapeDtypeStruct((nk, C), BF16),
        ),
        in_specs=[SMEM, whole(*kv.shape), whole(*tx.shape), block(per, HALF, D)],
        out_specs=(
            block(1, nk, QB),
            block(per, C // 2, D),
            block(1, C, QB),
            block(1, 1, QB),
            whole(nk, D),
            whole(D, nk),
            whole(nk, C),
        ),
        scratch_shapes=[pltpu.VMEM((C, nk), BF16), pltpu.VMEM((nk, QB), F32)],
        compiler_params=pltpu.CompilerParams(
            dimension_semantics=("arbitrary",), vmem_limit_bytes=LIMIT
        ),
        name="forward",
    )(guidance, kv, tx, q)


def own_tokens(x):
    a, b = pack_pair(x)
    return jnp.where(lax.axis_index("cfg") == 0, a, b)


def middle_kernel(
    S, NI, guidance, rate, msg, noise, old, reward,
    g_all, ratio, factor,
    got, g_own, part, parts, pair, rewards, s1, r1, s2, r2, ls, s3, r3, s4, r4, s5, r5,
):
    c, i, s = lax.axis_index("cfg"), lax.axis_index("img"), lax.axis_index("seq")
    barrier = pltpu.get_barrier_semaphore()

    def greet(k, carry):
        pl.semaphore_signal(
            barrier, inc=1, device_id={"seq": lax.rem(s + k, S)}, device_id_type=MESH
        )
        return carry

    lax.fori_loop(1, S, greet, 0)
    pl.semaphore_signal(barrier, inc=1, device_id={"cfg": 1 - c}, device_id_type=MESH)
    for k in range(1, NI):
        pl.semaphore_signal(
            barrier, inc=1, device_id={"img": lax.rem(i + k, NI)}, device_id_type=MESH
        )
    pl.semaphore_wait(barrier, S - 1 + 1 + NI - 1)

    def contribute(k, carry):
        t = lax.rem(s + k, S)
        away(msg.at[t], got.at[s], s1, r1, {"seq": t}).start()
        return carry

    lax.fori_loop(1, S, contribute, 0)
    for k in range(1, NI):
        away(reward, rewards.at[i], s5, r5, {"img": lax.rem(i + k, NI)}).start()
    noise_own = own_tokens(noise[...])
    old_own = own_tokens(old[...])
    drain(got.at[pl.ds(0, S - 1)], r1)
    got[s] = msg[s]
    guided = jnp.sum(got[...].astype(F32), axis=0)
    step = rate[0, 0]
    deviation = step * (guided - old_own)
    g_own[...] = (noise_own - deviation).astype(BF16)
    partial = jnp.sum(noise_own * deviation - 0.5 * deviation * deviation)
    part[...] = jnp.full(part.shape, partial, F32)
    mine = pltpu.make_async_copy(g_own, g_all.at[s], ls)
    mine.start()

    def share(k, carry):
        t = lax.rem(s + k, S)
        away(g_own, g_all.at[s], s2, r2, {"seq": t}).start()
        return carry

    lax.fori_loop(1, S, share, 0)

    def tell(k, carry):
        t = lax.rem(s + k, S)
        away(part, parts.at[s], s3, r3, {"seq": t}).start()
        return carry

    lax.fori_loop(1, S, tell, 0)
    drain(parts.at[pl.ds(0, S - 1)], r3)
    parts[s] = part[...]
    pair[0] = jnp.sum(parts[...], axis=0)
    swap = away(pair.at[0], pair.at[1], s4, r4, {"cfg": 1 - c})
    swap.start()
    if NI > 1:
        drain(rewards.at[pl.ds(0, NI - 1)], r5)
    rewards[i] = reward[...]
    mean = jnp.sum(rewards[...], axis=0) / NI
    square = jnp.sum(rewards[...] * rewards[...], axis=0) / NI
    spread_of = jnp.sqrt(jnp.maximum(square - mean * mean, 0.0))
    advantage = (reward[...] - mean) / jnp.maximum(spread_of, 1.0)
    swap.wait()
    log_ratio = (pair[0] + pair[1]) / (2 * S * HALF * C)
    ratio_now = jnp.exp(log_ratio)
    clipped = jnp.clip(ratio_now, 0.8, 1.2)
    keep = ratio_now * advantage <= clipped * advantage
    gain = jnp.where(keep, -ratio_now * advantage, 0.0)
    ratio[...] = ratio_now
    share_of = jnp.where(lax.rem(s, 2) == 0, guidance[0, 0], 1.0 - guidance[0, 0])
    factor[...] = gain * (step * share_of)
    mine.wait()
    drain(g_all.at[pl.ds(0, S - 1)], r2)
    drain(got.at[pl.ds(0, S - 1)], s1)
    drain(g_all.at[pl.ds(0, S - 1)], s2)
    drain(parts.at[pl.ds(0, S - 1)], s3)
    if NI > 1:
        drain(rewards.at[pl.ds(0, NI - 1)], s5)


def middle(S, NI, guidance, rate, msg, noise, old, reward):
    dma = pltpu.SemaphoreType.DMA
    tile = (8, D)
    return pl.pallas_call(
        functools.partial(middle_kernel, S, NI),
        out_shape=(
            jax.ShapeDtypeStruct((S, C // 2, D), BF16),
            jax.ShapeDtypeStruct(tile, F32),
            jax.ShapeDtypeStruct(tile, F32),
        ),
        in_specs=[SMEM, SMEM, VMEM, VMEM, VMEM, VMEM],
        out_specs=(ANY, VMEM, VMEM),
        scratch_shapes=[
            pltpu.VMEM((S, C // 2, D), BF16),
            pltpu.VMEM((C // 2, D), BF16),
            pltpu.VMEM(tile, F32),
            pltpu.VMEM((S, *tile), F32),
            pltpu.VMEM((2, *tile), F32),
            pltpu.VMEM((NI, *tile), F32),
            *([dma] * 11),
        ],
        compiler_params=pltpu.CompilerParams(collective_id=1, has_side_effects=True),
        name="middle",
    )(guidance, rate, msg, noise, old, reward)


def backward_kernel(
    S, factor, e_in, q, g, out_t, linv, keys_t, narrow,
    dq, own, oth, town, toth,
    gk, gv,
):
    nk = narrow.shape[0]
    step = pl.program_id(0)

    @pl.when(step == 0)
    def _():
        gk[...] = jnp.zeros_like(gk)
        gv[...] = jnp.zeros_like(gv)

    queries = q[...].reshape(QB, D)
    g_t = jnp.concatenate(
        [unpack_pair(g[2 * m].astype(F32), g[2 * m + 1].astype(F32)) for m in range(QB // D)], axis=1
    )
    gl_t = (g_t * linv[0]).astype(BF16)
    gl32 = gl_t.astype(F32)
    delta = jnp.sum(gl32 * out_t[0], axis=0, keepdims=True)
    gl_both = jnp.concatenate([gl32, gl32], axis=0).T.astype(BF16)
    dq_t = jnp.zeros((D, QB), F32)
    for at, size in chunks(nk):
        rows = slice(at, at + size)
        e = e_in[0, rows]
        gp = jnp.dot(narrow[rows], gl_t, preferred_element_type=F32)
        ds = (e.astype(F32) * (gp - delta)).astype(BF16)
        gv[rows] += jnp.dot(e, gl_both, preferred_element_type=F32)
        gk[rows] += jnp.dot(ds, queries, preferred_element_type=F32)
        dq_t = dq_t + jnp.dot(keys_t[:, rows], ds, preferred_element_type=F32)
    f = factor[0:1, 0:1]
    fs = f * D ** (-0.5)
    dq[...] = (dq_t * fs).T.astype(BF16).reshape(dq.shape)

    @pl.when(step == pl.num_programs(0) - 1)
    def _():
        third = HALF // 2
        n = third * S
        for p, out in ((0, own), (1, oth)):
            base = 2 * p * n
            for ab in range(2):
                rows = gk[base + ab * n : base + ab * n + n]
                out[:, third * ab : third * ab + third, :] = (rows * fs).astype(out.dtype).reshape(S, third, D)
            a, b = gv[base : base + n], gv[base + n : base + 2 * n]
            both = jnp.where(iota(a.shape, 1) < C, a, b) * f
            out[:, HALF:, :] = both.astype(out.dtype).reshape(S, third, D)
        H = S // 2
        for p, out in ((0, town), (1, toth)):
            base = 4 * n + p * H * TXT
            k = (gk[base : base + H * TXT] * fs).reshape(H, TXT, D)
            v = gv[base : base + H * TXT]
            v = (jnp.where(iota(v.shape, 1) < C, v, 0.0) * f).reshape(H, TXT, D)
            out[...] = jnp.concatenate([k, v], axis=1).astype(out.dtype)


def backward(S, factor, e, q, g, out_t, linv, keys_t, narrow):
    nb, nk, _ = e.shape
    H = S // 2
    per = QB // HALF
    whole = lambda *shape: pl.BlockSpec(shape, lambda i: (0,) * len(shape))
    block = lambda *shape: pl.BlockSpec(shape, lambda i: (i,) + (0,) * (len(shape) - 1))
    rows = HALF + HALF // 2
    return pl.pallas_call(
        functools.partial(backward_kernel, S),
        grid=(nb,),
        out_shape=(
            jax.ShapeDtypeStruct((S, HALF, D), BF16),
            jax.ShapeDtypeStruct((S, rows, D), F32),
            jax.ShapeDtypeStruct((S, rows, D), BF16),
            jax.ShapeDtypeStruct((H, 2 * TXT, D), F32),
            jax.ShapeDtypeStruct((H, 2 * TXT, D), BF16),
        ),
        in_specs=[
            whole(8, D),
            block(1, nk, QB),
            block(per, HALF, D),
            block(per, C // 2, D),
            block(1, C, QB),
            block(1, 1, QB),
            whole(D, nk),
            whole(nk, C),
        ],
        out_specs=(
            block(per, HALF, D),
            whole(S, rows, D),
            whole(S, rows, D),
            whole(H, 2 * TXT, D),
            whole(H, 2 * TXT, D),
        ),
        scratch_shapes=[pltpu.VMEM((nk, D), F32), pltpu.VMEM((nk, D), F32)],
        compiler_params=pltpu.CompilerParams(
            dimension_semantics=("arbitrary",), vmem_limit_bytes=LIMIT
        ),
        name="backward",
    )(factor, e, q, g, out_t, linv, keys_t, narrow)


def home_kernel(
    S, NI, dq, own, oth, town, toth, img, tx, rt,
    grad, tgrad, rg,
    vbuf, xu, xk, xt, uf, kf, tf, ub, tb, dv, rgp, r1, a1, r2, a2, r3, a3, r4,
    vsem, dvsem, xs, xr, us, ur, ts, tr, qs, qr, ks, kr, as_, ar, ls,
):
    H = S // 2
    ZN = S // YN
    NP = 2 * NI
    HD = rgp.shape[1]
    W = HD // NP
    third = HALF // 2
    c, i, s = lax.axis_index("cfg"), lax.axis_index("img"), lax.axis_index("seq")
    head, branch = s // 2, lax.rem(s, 2)
    y, z = lax.rem(s, YN), s // YN
    me = 2 * i + c
    barrier = signal_plane(S)
    for k in range(1, NI):
        for core in range(2):
            pl.semaphore_signal(
                barrier,
                inc=1,
                device_id={"cfg": core, "img": lax.rem(i + k, NI)},
                device_id_type=MESH,
            )
    vcopy = pltpu.make_async_copy(img.at[2], vbuf, vsem)
    vcopy.start()
    pl.semaphore_wait(barrier, 2 * S - 1 + 2 * (NI - 1))
    other = {"cfg": 1 - c}
    swaps = [
        away(oth.at[:, pl.ds(HALF, third)], xu, xs.at[0], xr.at[0], other),
        away(toth, xt, xs.at[1], xr.at[1], other),
        away(oth.at[:, pl.ds(0, HALF)], xk, xs.at[2], xr.at[2], other),
    ]
    for w in swaps:
        w.start()
    cols = pl.ds(pl.multiple_of(head * D, D), D)
    mine = pl.ds(pl.multiple_of(HALF * c, HALF), HALF)
    swaps[0].wait_recv()
    uf[...] = (own[:, HALF:, :] + xu[...].astype(F32)).astype(BF16)
    swaps[1].wait_recv()
    tf[...] = (town[...] + xt[...].astype(F32)).astype(BF16)

    def send_u(k, carry):
        t = lax.rem(s + k, S)
        put(uf.at[t], ub.at[head, c], us, ur, branch, t)
        return carry

    lax.fori_loop(0, S, send_u, 0)

    def send_text(k, carry):
        put(tf.at[k], tb.at[head], ts, tr, branch, c * H + k)
        return carry

    lax.fori_loop(0, H, send_text, 0)

    def send_queries(k, carry):
        t = lax.rem(s + k, S)
        put(dq.at[t], grad.at[0, mine, cols], qs, qr, branch, t)
        return carry

    lax.fori_loop(0, S, send_queries, 0)
    swaps[2].wait_recv()
    kf[...] = (own[:, :HALF, :] + xk[...].astype(F32)).astype(BF16)

    def send_keys(k, carry):
        t = lax.rem(s + k, S)
        put(kf.at[t], grad.at[1, mine, cols], ks, kr, branch, t)
        return carry

    lax.fori_loop(0, S, send_keys, 0)
    vcopy.wait()
    drain(ub, ur)
    drain(tb, tr)

    def widen(h, carry):
        at = pl.ds(pl.multiple_of(h * D, D), D)
        r = rt[:, at]
        twice = jnp.concatenate([r, r], axis=0)
        low = iota((third, D), 1) < C
        u0, u1 = ub[h, 0].astype(F32), ub[h, 1].astype(F32)
        t = tb[h].astype(F32)
        text = jnp.where(iota(t.shape, 0) < TXT, 0.0, t)
        spaced = jnp.concatenate(
            [
                jnp.where(low, u0, 0.0),
                jnp.where(low, 0.0, u0),
                jnp.where(low, u1, 0.0),
                jnp.where(low, 0.0, u1),
                text,
            ],
            axis=0,
        )
        wide = jnp.dot(spaced.astype(BF16), twice, preferred_element_type=F32)
        dv[:, at] = wide[: 2 * HALF].astype(BF16)
        tgrad[:, at] = jnp.where(iota(t.shape, 0) < TXT, t, wide[2 * HALF :]).astype(BF16)
        values = jnp.concatenate([vbuf[:, at], tx[:, at]], axis=0)
        res = jnp.dot(spaced.T.astype(BF16), values, preferred_element_type=F32)
        rgp[:, at] = res[:C] + res[C:]
        return carry

    lax.fori_loop(0, H, widen, 0)
    dvcopy = pltpu.make_async_copy(dv, grad.at[2], dvsem)
    dvcopy.start()

    def peers():
        for k in range(1, NP):
            p = lax.rem(me + k, NP)
            yield p, {"cfg": lax.rem(p, 2), "img": p // 2}

    def piece(p):
        return pl.ds(pl.multiple_of(p * W, D), W)

    for p, device in peers():
        away(rgp.at[:, piece(p)], r1.at[me], as_.at[0], ar.at[0], device).start()
    drain(r1.at[pl.ds(0, NP - 1)], ar.at[0])
    r1[me] = rgp[:, piece(me)]
    a1[...] = jnp.sum(r1[...], axis=0)
    RY = C // YN

    def strip(n):
        return pl.ds(pl.multiple_of(n * RY, 8), RY)

    for k in range(1, YN):
        n = lax.rem(y + k, YN)
        away(a1.at[strip(n)], r2.at[y], as_.at[1], ar.at[1], {"seq": z * YN + n}).start()
    drain(r2.at[pl.ds(0, YN - 1)], ar.at[1])
    r2[y] = a1[strip(y), :]
    a2[...] = jnp.sum(r2[...], axis=0)
    for k in range(1, ZN):
        n = lax.rem(z + k, ZN)
        away(a2, r3.at[z], as_.at[2], ar.at[2], {"seq": n * YN + y}).start()
    drain(r3.at[pl.ds(0, ZN - 1)], ar.at[2])
    r3[z] = a2[...]
    a3[...] = jnp.sum(r3[...], axis=0)
    for k in range(1, YN):
        n = lax.rem(y + k, YN)
        away(a3, r4.at[y], as_.at[3], ar.at[3], {"seq": z * YN + n}).start()
    drain(r4.at[pl.ds(0, YN - 1)], ar.at[3])
    r4[y] = a3[...]
    keep = pltpu.make_async_copy(r4, rg.at[:, :, piece(me)], ls)
    keep.start()
    for p, device in peers():
        away(r4, rg.at[:, :, piece(me)], as_.at[4], ar.at[4], device).start()

    keep.wait()
    drain(r1.at[pl.ds(0, NP - 1)], ar.at[4])
    dvcopy.wait()
    drain(grad.at[0], qr)
    drain(grad.at[1], kr)
    for w in swaps:
        w.wait_send()
    drain(r1.at[pl.ds(0, NP - 1)], as_.at[0])
    drain(r2.at[pl.ds(0, YN - 1)], as_.at[1])
    drain(r3.at[pl.ds(0, ZN - 1)], as_.at[2])
    drain(r4.at[pl.ds(0, YN - 1)], as_.at[3])
    drain(r1.at[pl.ds(0, NP - 1)], as_.at[4])

    text_here = jnp.logical_and(branch == c, s // H == c)

    @pl.when(branch == c)
    def _():
        drain(uf.at[pl.ds(0, S - 1)], us)
        drain(dq.at[pl.ds(0, S - 1)], qs)
        drain(kf.at[pl.ds(0, S - 1)], ks)

    @pl.when(branch != c)
    def _():
        drain(uf, us)
        drain(dq, qs)
        drain(kf, ks)

    @pl.when(text_here)
    def _():
        drain(tf.at[pl.ds(0, H - 1)], ts)

    @pl.when(jnp.logical_not(text_here))
    def _():
        drain(tf, ts)


def home(S, NI, dq, own, oth, town, toth, img, tx, rt):
    H = S // 2
    HD = rt.shape[1]
    NP = 2 * NI
    W = HD // NP
    RY = C // YN
    third = HALF // 2
    dma = pltpu.SemaphoreType.DMA
    return pl.pallas_call(
        functools.partial(home_kernel, S, NI),
        out_shape=(
            jax.ShapeDtypeStruct(img.shape, BF16),
            jax.ShapeDtypeStruct((2 * TXT, HD), BF16),
            jax.ShapeDtypeStruct((YN, RY, HD), F32),
        ),
        in_specs=[ANY, VMEM, ANY, VMEM, ANY, ANY, VMEM, VMEM],
        out_specs=(ANY, VMEM, ANY),
        scratch_shapes=[
            pltpu.VMEM(img.shape[1:], BF16),
            pltpu.VMEM((S, third, D), BF16),
            pltpu.VMEM((S, HALF, D), BF16),
            pltpu.VMEM((H, 2 * TXT, D), BF16),
            pltpu.VMEM((S, third, D), BF16),
            pltpu.VMEM((S, HALF, D), BF16),
            pltpu.VMEM((H, 2 * TXT, D), BF16),
            pltpu.VMEM((H, 2, third, D), BF16),
            pltpu.VMEM((H, 2 * TXT, D), BF16),
            pltpu.VMEM(img.shape[1:], BF16),
            pltpu.VMEM((C, HD), F32),
            pltpu.VMEM((NP, C, W), F32),
            pltpu.VMEM((C, W), F32),
            pltpu.VMEM((YN, RY, W), F32),
            pltpu.VMEM((RY, W), F32),
            pltpu.VMEM((S // YN, RY, W), F32),
            pltpu.VMEM((RY, W), F32),
            pltpu.VMEM((YN, RY, W), F32),
            dma,
            dma,
            dma((3,)),
            dma((3,)),
            *([dma] * 8),
            dma((5,)),
            dma((5,)),
            dma,
        ],
        compiler_params=pltpu.CompilerParams(
            collective_id=2, has_side_effects=True, vmem_limit_bytes=LIMIT
        ),
        name="home",
    )(dq, own, oth, town, toth, img, tx, rt)


def on_device(S, NI, img_qkv, txt_kv, readout, old_velocity, noise, step_ratio, rewards, guidance):
    img = img_qkv[0, 0].transpose(1, 0, 2)
    text = txt_kv[0, 0]
    tx = jnp.concatenate([text[:, 0], text[:, 1]], axis=0)
    rt = readout.T
    scalar = lambda x: x.reshape(1, 1)
    kv, q, txo = spread(S, img, tx, rt)
    e, msg, out_t, linv, keys, keys_t, narrow = forward(S, scalar(guidance), kv, txo, q)
    reward = jnp.broadcast_to(scalar(rewards), (8, D))
    g, ratio, factor = middle(
        S, NI, scalar(guidance), scalar(step_ratio), msg, noise[0].T, old_velocity[0].T, reward
    )
    dq, own, oth, town, toth = backward(S, factor, e, q, g, out_t, linv, keys_t, narrow)
    grad, tgrad, rg = home(S, NI, dq, own, oth, town, toth, img, tx, rt)
    img_grad = grad.transpose(1, 0, 2)[None, None]
    txt_grad = jnp.stack([tgrad[:TXT], tgrad[TXT:]], axis=1)[None, None]
    return (img_grad, txt_grad, rg.reshape(C, -1).T, ratio[0, :1])


def solution(mesh):
    S, NI = mesh.shape["seq"], mesh.shape["img"]
    placed = (
        P("cfg", "img", "seq", None, None),
        P("cfg", "img", "seq", None, None),
        P(),
        P("img", "seq", None),
        P("img", "seq", None),
        P("img"),
        P("img"),
        P(),
    )
    return jax.shard_map(
        functools.partial(on_device, S, NI),
        mesh=mesh,
        in_specs=placed,
        out_specs=(
            P("cfg", "img", "seq", None, None),
            P("cfg", "img", "seq", None, None),
            P(),
            P("img"),
        ),
        check_vma=False,
    )
```

time: 420 us -> 202 us (0.48); the launches traced: 412 us -> 200 us
  Pallas kernels: 0 us -> 189 us
  waiting for transfers between devices: 108 us -> 0 us
  matrix products: 72.3 us -> 0 us
  blocking collectives: 69.8 us -> 0 us
  other arithmetic: 65.8 us -> 0.64 us
  starting transfers between devices: 52.2 us -> 0 us
  local copies, waits for them, and re-layouts: 36 us -> 7.72 us
  between operations: 7.66 us -> 2.62 us
    pallas_call x0 -> x5, Pallas kernels: none -> 189 us  [the longest x1 56 us: home(): pl.pallas_call(functools.partial(home_kernel, S, NI), out_shape=(jax.Shap...]
    dot_general x27 -> x0, matrix products: 72.3 us -> none  [the longest x4 19.7 us: one_block(): jnp.einsum('hqk,qhd->khd', prob, grad_block, preferred_element_type=jnp.f...]
    all_to_all x3 -> x0, blocking collectives: 69.8 us -> none  [the longest x1 42.2 us: side_by_side(): lax.all_to_all(both, axis, split_axis=split_dim, concat_axis=concat_dim,...]
    all_to_all x8 -> x0, waiting for transfers between devices: 68 us -> none  [the longest x1 29.8 us: side_by_side(): lax.all_to_all(both, axis, split_axis=split_dim, concat_axis=concat_dim,...]
    all_to_all x8 -> x0, starting transfers between devices: 45.1 us -> none  [the longest x4 20.7 us: from_everyone(): return lax.all_to_all(copies, axis, split_axis=0, concat_axis=0, tiled=True)]
    ppermute x5 -> x0, waiting for transfers between devices: 40.1 us -> none  [swapped(): return lax.ppermute(block, axis, route)]
    convert_element_type x6 -> x0, other arithmetic: 27.8 us -> none  [the longest x4 26.3 us: one_block(): grad_scores = (weights * (grad_probs - delta) * scale).astype(jnp.bfloat16)]
    dynamic_update_slice x4 -> x0, other arithmetic: 14.9 us -> none  [attend_forward(): probs, mixed = lax.map(one_block, query_blocks)]
  transfers between devices with their start and end apart: 13 -> 0, of which waited for: 9 -> 0; matrix products, arithmetic and copies ran while one was open for 35% -> 0% of each run, Pallas kernels for 0% -> 0%
where the time goes in v1:
time: 202 us; the launch traced here: 200 us
  Pallas kernels  189 us (94%)
  local copies, waits for them, and re-layouts  7.72 us (4%)
  between operations  2.62 us (1%)
    pallas_call x1, Pallas kernels, home(): pl.pallas_call(functools.partial(home_kernel, S, NI), out_shape=(jax.Shap...  56 us
    pallas_call x1, Pallas kernels, spread(): pl.pallas_call(functools.partial(spread_kernel, S), out_shape=(jax.ShapeD...  46.2 us
    pallas_call x1, Pallas kernels, middle(): pl.pallas_call(functools.partial(middle_kernel, S, NI), out_shape=(jax.Sh...  30.3 us
    pallas_call x1, Pallas kernels, backward(): pl.pallas_call(functools.partial(backward_kernel, S), grid=(nb,), out_sha...  29.6 us
    pallas_call x1, Pallas kernels, forward(): pl.pallas_call(functools.partial(forward_kernel, S), grid=(nb,), out_shap...  26.8 us
    unnamed x6, local copies, waits for them, and re-layouts  5.14 us

profile of v1, /device:TPU:5, one launch (start us, length us, event | category | flops | bytes accessed | tf_op | source)
XLA Modules:
  0.0 199.8 jit_solution(481593576073454352)
XLA Ops:
  2.6 0.6 broadcast_in_dim.14.reward
  3.2 0.9 copy.15
  4.0 0.6 pad_maximum_fusion.tx
  4.7 46.2 %spread.1 = (bf16[2,32,96,128]{3,2,1,0:T(8,128)(2,1)}, bf16[32,64,128]{2,1,0:T(8,128)(2,1)}, bf16[2,16,16,128]{3,2,1,0:T(8,128)(2,1)}) custom-call(bf16[3,128,2048]{2,1,0:T(8,128)(2,1)} %bitcast.37, bf16[16,2048]{1,0:T(8,128)(2,1)} %pad_maximum_fusion.tx, bf16[64,2048]{1,0:T(8,128)(2,1)} %bitcast.40), custom_call_target="tpu_custom_call" | custom-call | tf_op jit(solution)/shard_map/spread/pallas_call | solution.py:172
  50.9 26.8 %forward.1 = (bf16[8,4352,256]{2,1,0:T(8,128)(2,1)}, bf16[32,32,128]{2,1,0:T(8,128)(2,1)}, f32[8,64,256]{2,1,0:T(8,128)}, f32[8,1,256]{2,1,0:T(1,128)}, bf16[435...) custom-call(f32[1,1]{1,0:T(1,128)} %bitcast.35.guidance, ...), custom_call_target="tpu_custom_call" | custom-call | tf_op jit(solution)/shard_map/forward/pallas_call | solution.py:283
  77.7 30.3 %middle.1 = (bf16[32,32,128]{2,1,0:T(8,128)(2,1)}, f32[8,128]{1,0:T(8,128)}, f32[8,128]{1,0:T(8,128)}) custom-call(f32[1,1]{1,0:T(1,128)} %bitcast.36.guidance, f32[1,1]{1,0:T(1,128)} %bitcast.33.rate, bf16[32,32,128]{2,1,0:T(8,128)(2,1)} %get-tuple-element.27.msg, f32[64,128]{1,0:T(8,128)} %bitcast.44, f32[64,128]{1,0:T(8,128)} %bitcast.45, ...), custom_call_target="tpu_custom_call" | custom-call | tf_op jit(solution)/shard_map/middle/pallas_call | solution.py:407
  108.0 1.2 slice.19
  109.2 29.6 %backward.1 = (bf16[32,64,128]{2,1,0:T(8,128)(2,1)}, f32[32,96,128]{2,1,0:T(8,128)}, bf16[32,96,128]{2,1,0:T(8,128)(2,1)}, f32[16,16,128]{2,1,0:T(8,128)}, bf16[16,16,128]{2,1,0:T(8,128)(2,1)}) custom-call(f32[8,128]{1,0:T(8,128)} %get-tuple-element.28.factor, bf16[8,4352,256]{2,1,0:T(8,128)(2,1)} %get-tuple-element.29.e_in, ...), custom_call_target="tpu_custom_call" | custom-call | tf_op jit(solution)/shard_map/backward/pallas_call | solution.py:492
  138.8 56.0 %home.1 = (bf16[3,128,2048]{2,1,0:T(8,128)(2,1)}, bf16[16,2048]{1,0:T(8,128)(2,1)}, f32[4,16,2048]{2,1,0:T(8,128)}) custom-call(bf16[32,64,128]{2,1,0:T(8,128)(2,1)} %get-tuple-element.35.dq, f32[32,96,128]{2,1,0:T(8,128)} %get-tuple-element.36.own, bf16[32,96,128]{2,1,0:T(8,128)(2,1)} %get-tuple-element.37.oth, f32[16,16,128]{2,1,0:T(8,128)} %get-tuple-element.38.town, ...), custom_call_target="tpu_custom_call" | custom-call | tf_op jit(solution)/shard_map/home/pallas_call | solution.py:716
  194.8 0.8 slice_bitcast_fusion.3
  195.6 0.7 copy.13
  196.3 0.0 copy-start
  196.3 2.8 %copy.21 = bf16[1,1,128,3,2048]{4,2,3,1,0:T(8,128)(2,1)} copy(bf16[1,1,128,3,2048]{4,2,3,1,0:T(8,128)(2,1)} %bitcast.39) | data formatting | bytes 3145728
  199.0 0.0 copy-done
  199.1 0.8 copy.22
  (2 shorter events, 0.0 us)
Async XLA Ops:
  196.3 2.8 %copy-start = (f32[4,16,2048]{2,1,0:T(8,128)S(1)}, f32[4,16,2048]{2,1,0:T(8,128)}, u32[]{:S(2)}) copy-start(f32[4,16,2048]{2,1,0:T(8,128)} %get-tuple-element.42) | copy-start | bytes 1572868

commit v2 on v0

v2 whole, which is shorter than its diff:
```python
import functools

import jax
import jax.numpy as jnp
from jax import lax
from jax.experimental import pallas as pl
from jax.experimental.pallas import tpu as pltpu
from jax.sharding import PartitionSpec as P

D = 128
C = 64
HALF = 64
TXT = 8
YN = 4
QB = 256
KB = 1024
SB = 256
ONES = 16
MESH = pl.DeviceIdType.MESH
F32 = jnp.float32
BF16 = jnp.bfloat16
NT = (((1,), (1,)), ((), ()))
TN = (((0,), (0,)), ((), ()))
ANY = pl.BlockSpec(memory_space=pl.ANY)
VMEM = pl.BlockSpec(memory_space=pltpu.VMEM)
SMEM = pl.BlockSpec(memory_space=pltpu.SMEM)
LIMIT = 60 * 1024 * 1024


def iota(shape, dim):
    return lax.broadcasted_iota(jnp.int32, shape, dim)


def put(src, dst, send, recv, core, chip):
    here = jnp.logical_and(core == lax.axis_index("cfg"), chip == lax.axis_index("seq"))

    @pl.when(here)
    def _():
        pltpu.make_async_copy(src, dst, recv).start()

    @pl.when(jnp.logical_not(here))
    def _():
        away(src, dst, send, recv, {"cfg": core, "seq": chip}).start()


def away(src, dst, send, recv, device):
    return pltpu.make_async_remote_copy(
        src_ref=src,
        dst_ref=dst,
        send_sem=send,
        recv_sem=recv,
        device_id=device,
        device_id_type=MESH,
    )


def drain(ref, sem):
    pltpu.make_async_copy(ref, ref, sem).wait()


def signal_plane(chips):
    c, s = lax.axis_index("cfg"), lax.axis_index("seq")
    barrier = pltpu.get_barrier_semaphore()

    def one(k, carry):
        n = lax.rem(c * chips + s + k, 2 * chips)
        pl.semaphore_signal(
            barrier,
            inc=1,
            device_id={"cfg": n // chips, "seq": lax.rem(n, chips)},
            device_id_type=MESH,
        )
        return carry

    lax.fori_loop(1, 2 * chips, one, 0)
    return barrier


def pack_pair(x):
    top, low = x[: C // 2], x[C // 2 :]
    lower = iota(top.shape, 1) < HALF
    return (
        jnp.where(lower, top, pltpu.roll(low, HALF, 1)),
        jnp.where(lower, pltpu.roll(top, HALF, 1), low),
    )


def unpack_pair(a, b):
    lower = iota(a.shape, 1) < HALF
    return jnp.concatenate(
        [jnp.where(lower, a, pltpu.roll(b, HALF, 1)), jnp.where(lower, pltpu.roll(a, HALF, 1), b)], axis=0
    )


def own_tokens(x):
    a, b = pack_pair(x)
    return jnp.where(lax.axis_index("cfg") == 0, a, b)


def step_kernel(
    S, NI, guidance, rate, img, tx, rt, noise, old, reward,
    grad, tgrad, rg, ratio,
    vbuf, vrp, txb, kv, text, qbuf, keys, keys_t, narrow, narrow_t, scores_a, scores_b, hold_0, hold_1, hold_2, hold_3, hold_text, weights, out_t, linv,
    msg, got, g_own, g_all, part, parts, pair, rewards, gl, delta, gk, gv,
    uo, xu, uf, uto, xut, utf, ko, xk, kf, kto, xkt, ktf, dqb, ub, utb, ktb, dv, rgp, r1, a1, r2, a2, r3, a3, r4,
    vsem, ks, kr, qs, qr, ts, tr, fs, fr, fts, ftr, ms, mr, gs, gr, ps, pr, pairs, pairr, rs, rr,
    xs, xr, us, ur, uts, utr, dqs, dqr, dks, dkr, kts, ktr, dvsem, as_, ar, ls,
):
    H = S // 2
    ZN = S // YN
    NP = 2 * NI
    W = rgp.shape[1] // NP
    RY = C // YN
    NK = keys.shape[0]
    NKI = 2 * HALF * S
    holds = (hold_0, hold_1, hold_2, hold_3)[: min(KB, NKI) // SB]
    third = HALF // 2
    n3 = third * S
    c, i, s = lax.axis_index("cfg"), lax.axis_index("img"), lax.axis_index("seq")
    head, branch = s // 2, lax.rem(s, 2)
    y, z = lax.rem(s, YN), s // YN
    me = 2 * i + c
    other = {"cfg": 1 - c}

    vcopy = pltpu.make_async_copy(img.at[2], vbuf, vsem)
    vcopy.start()
    barrier = signal_plane(S)
    for k in range(1, NI):
        for core in range(2):
            pl.semaphore_signal(
                barrier, inc=1, device_id={"cfg": core, "img": lax.rem(i + k, NI)}, device_id_type=MESH
            )
    vcopy.wait()

    def squeeze(h, carry):
        cols = pl.ds(pl.multiple_of(h * D, D), D)
        r = rt[:, cols]
        twice = jnp.concatenate([r, r], axis=0)
        x = lax.dot_general(vbuf[:, cols], twice, NT, preferred_element_type=F32)
        low = iota((third, D), 1) < C
        for j in range(2):
            first = x[HALF * j : HALF * j + third]
            second = x[HALF * j + third : HALF * j + HALF]
            vrp[h, j] = jnp.where(low, first, second).astype(BF16)
        t = tx[:, cols]
        yv = lax.dot_general(t, twice, NT, preferred_element_type=F32)
        yv = jnp.where(iota(yv.shape, 1) < C, yv, 0.0)
        txb[h] = jnp.where(iota(yv.shape, 0) < TXT, t.astype(F32), yv).astype(BF16)
        return carry

    lax.fori_loop(0, H, squeeze, 0)
    pl.semaphore_wait(barrier, 2 * S - 1 + 2 * (NI - 1))

    side = s // H

    def at_distance(n, sign):
        far = (n + 1) // 2
        return lax.rem(z + jnp.where(lax.rem(n, 2) == 1, sign * far, -sign * far) + ZN, ZN)

    def send_keys(k, carry):
        zt = at_distance(k // 2, 1)
        h = 2 * zt + lax.rem(k, 2)
        chip = 2 * h + c
        cols = pl.ds(pl.multiple_of(h * D, D), D)
        for j in range(2):
            put(img.at[1, pl.ds(HALF * j, HALF), cols], kv.at[0, s, pl.ds(0, HALF)], ks.at[h, j], kr.at[s], j, chip)
            put(vrp.at[h, j], kv.at[0, s, pl.ds(HALF, third)], ks.at[h, j], kr.at[s], j, chip)
        put(txb.at[h], text.at[0, lax.rem(s, H)], ts.at[h], tr.at[lax.rem(s, H)], side, chip)
        return carry

    lax.fori_loop(0, H, send_keys, 0)

    def send_queries(k, carry):
        zt = at_distance(k // 2, 1)
        h = 2 * zt + lax.rem(k, 2)
        chip = 2 * h + c
        cols = pl.ds(pl.multiple_of(h * D, D), D)
        for j in range(2):
            put(img.at[0, pl.ds(HALF * j, HALF), cols], qbuf.at[s], qs.at[h, j], qr.at[s], j, chip)
        return carry

    lax.fori_loop(0, H, send_queries, 0)
    for k in range(1, NI):
        away(reward, rewards.at[i], rs, rr, {"img": lax.rem(i + k, NI)}).start()

    narrow_t[C:] = jnp.where(iota((ONES, NK), 0) == 0, 1.0, 0.0).astype(BF16)

    def lay_out(p, zs):
        four = pl.ds(zs * YN, YN)
        packed = kv[p, four, HALF:, :].reshape(third * YN, D)
        turned = packed.astype(F32).T
        for ab in range(2):
            rows = pl.ds(pl.multiple_of((2 * p + ab) * n3 + zs * (third * YN), third * YN), third * YN)
            block = kv[p, four, third * ab : third * ab + third, :].reshape(third * YN, D)
            keys[rows, :D] = block
            keys[rows, D:] = block
            keys_t[:, rows] = block.astype(F32).T.astype(BF16)
            one = turned[C * ab : C * ab + C]
            narrow_t[:C, rows] = one.astype(BF16)
            narrow[rows] = jnp.concatenate([one, one], axis=0).T.astype(BF16)

    def arrive(n, carry):
        zs = at_distance(n, -1)
        for yy in range(YN):
            src = zs * YN + yy
            drain(kv.at[0, src], kr.at[src])
            away(kv.at[0, src], kv.at[1, src], fs.at[src], fr.at[src], other).start()
        lay_out(0, zs)
        return carry

    lax.fori_loop(0, ZN, arrive, 0)

    def arrive_text(k, carry):
        drain(text.at[0, k], tr.at[k])
        away(text.at[0, k], text.at[1, k], fts.at[k], ftr.at[k], other).start()
        return carry

    lax.fori_loop(0, H, arrive_text, 0)

    def arrive_other(n, carry):
        zs = at_distance(n, -1)
        for yy in range(YN):
            drain(kv.at[1, zs * YN + yy], fr.at[zs * YN + yy])
        lay_out(1, zs)
        return carry

    lax.fori_loop(0, ZN, arrive_other, 0)

    def arrive_other_text(k, carry):
        drain(text.at[1, k], ftr.at[k])
        return carry

    lax.fori_loop(0, H, arrive_other_text, 0)
    words = text[...].astype(F32)
    tk = words[:, :, :TXT, :].reshape(TXT * S, D)
    tv = words[:, :, TXT:, :].reshape(TXT * S, D)
    last = pl.ds(NKI, TXT * S)
    keys[last, :D] = tk.astype(BF16)
    keys[last, D:] = tk.astype(BF16)
    keys_t[:, last] = tk.T.astype(BF16)
    tvt = tv.T[:C]
    narrow_t[:C, last] = tvt.astype(BF16)
    narrow[last] = jnp.concatenate([tvt, tvt], axis=0).T.astype(BF16)

    def over_keys(body, carry):
        for at in range(0, NK, SB):
            carry = body(slice(at, min(at + SB, NK)), carry)
        return carry

    def queries_t(zs):
        for yy in range(YN):
            drain(qbuf.at[zs * YN + yy], qr.at[zs * YN + yy])
        x = qbuf[pl.ds(zs * YN, YN)].reshape(QB, D).astype(F32).T * (D ** (-0.5) * 1.4426950408889634)
        hi = x.astype(BF16)
        return jnp.concatenate([hi, (x - hi.astype(F32)).astype(BF16)], axis=0)

    def score(buf, rows, q_t, top):
        st = jnp.dot(keys[rows], q_t, preferred_element_type=F32)
        buf[rows] = st
        return jnp.maximum(top, jnp.max(st.reshape(st.shape[0] // 8, 8, QB), axis=0))

    def weigh(buf, zs, rows, top, hold):
        e = jnp.exp2(buf[rows] - top).astype(BF16)
        weights[zs, rows] = e
        hold[...] = e

    def mix(rows, hold, mixed):
        return mixed + jnp.dot(narrow_t[:, rows], hold[...], preferred_element_type=F32)

    low_top = jnp.full((8, QB), -jnp.inf, F32)
    no_mix = jnp.zeros((C + ONES, QB), F32)
    branch_share = jnp.where(branch == 0, guidance[0, 0], 1.0 - guidance[0, 0])
    parts_of = NKI // KB
    subs = KB // SB

    def chunk(k, sub):
        return pl.ds(pl.multiple_of(k * KB + sub * SB, SB), SB)

    def first_scores(q_t):
        def body(k, t):
            for sub in range(subs):
                t = score(scores_a, chunk(k, sub), q_t, t)
            return t

        return score(scores_a, last, q_t, lax.fori_loop(0, parts_of, body, low_top))

    def attend(n, now, then, top8, ahead):
        zs = at_distance(n, -1)
        top = jnp.max(top8, axis=0, keepdims=True)
        q_t = queries_t(at_distance(n + 1, -1)) if ahead else None
        next8 = score(then, last, q_t, low_top) if ahead else low_top
        weigh(now, zs, last, top, hold_text)
        mixed = mix(last, hold_text, no_mix)
        holds[subs - 1][...] = jnp.zeros((SB, QB), BF16)

        def body(k, carry):
            next8, mixed = carry
            for sub in range(subs):
                before = chunk(jnp.maximum(k - 1, 0), subs - 1) if sub == 0 else chunk(k, sub - 1)
                mixed = mix(before, holds[sub - 1], mixed)
                if ahead:
                    next8 = score(then, chunk(k, sub), q_t, next8)
                weigh(now, zs, chunk(k, sub), top, holds[sub])
            return next8, mixed

        next8, mixed = lax.fori_loop(0, parts_of, body, (next8, mixed))
        mixed = mix(chunk(parts_of - 1, subs - 1), holds[subs - 1], mixed)
        inverse = 1.0 / mixed[C : C + 1]
        linv[zs] = inverse
        normal = mixed[:C] * inverse
        out_t[zs] = normal
        for m in range(QB // D):
            a, b = pack_pair(normal[:, D * m : D * m + D] * branch_share)
            for yy, part_of in ((2 * m, a), (2 * m + 1, b)):
                msg[zs * YN + yy] = part_of.astype(BF16)
        for yy in range(YN):
            t = zs * YN + yy
            put(msg.at[t], got.at[s], ms, mr, c, t)
        return next8

    top = first_scores(queries_t(at_distance(0, -1)))

    def two(m, top):
        top = attend(2 * m, scores_a, scores_b, top, True)
        return attend(2 * m + 1, scores_b, scores_a, top, True)

    top = lax.fori_loop(0, ZN // 2 - 1, two, top)
    if ZN > 1:
        top = attend(ZN - 2, scores_a, scores_b, top, True)
        attend(ZN - 1, scores_b, scores_a, top, False)
    else:
        attend(0, scores_a, scores_b, top, False)

    noise_own = own_tokens(noise[...])
    old_own = own_tokens(old[...])
    drain(got, mr)
    guided = jnp.sum(got[...].astype(F32), axis=0)
    step = rate[0, 0]
    deviation = step * (guided - old_own)
    g_own[...] = (noise_own - deviation).astype(BF16)

    def share(k, carry):
        t = at_distance(k // YN, 1) * YN + lax.rem(y + k, YN)
        put(g_own, g_all.at[s], gs, gr.at[s], c, t)
        return carry

    lax.fori_loop(0, S, share, 0)
    partial = jnp.sum(noise_own * deviation - 0.5 * deviation * deviation)
    part[...] = jnp.full(part.shape, partial, F32)

    def tell(k, carry):
        put(part, parts.at[s], ps, pr, c, lax.rem(s + k, S))
        return carry

    lax.fori_loop(0, S, tell, 0)

    gv[...] = jnp.zeros_like(gv)
    gk[...] = jnp.zeros_like(gk)

    def narrow_grads(n, carry):
        zs = at_distance(n, -1)
        for yy in range(YN):
            drain(g_all.at[zs * YN + yy], gr.at[zs * YN + yy])
        g_t = jnp.concatenate(
            [
                unpack_pair(g_all[zs * YN + 2 * m].astype(F32), g_all[zs * YN + 2 * m + 1].astype(F32))
                for m in range(QB // D)
            ],
            axis=1,
        )
        g_t = g_t * linv[zs]
        hi = g_t.astype(BF16)
        lo = (g_t - hi.astype(F32)).astype(BF16)
        gl[zs] = jnp.concatenate([hi, lo], axis=0)
        delta[zs] = jnp.sum((hi.astype(F32) + lo.astype(F32)) * out_t[zs], axis=0, keepdims=True)
        hi32 = hi.astype(F32)
        cols = jnp.concatenate([hi32, hi32], axis=0).T.astype(BF16)

        def one(rows, cr):
            gv[rows] += jnp.dot(weights[zs, rows], cols, preferred_element_type=F32)
            return cr

        return over_keys(one, carry)

    lax.fori_loop(0, ZN, narrow_grads, 0)

    drain(parts, pr)
    pair[0] = jnp.sum(parts[...], axis=0)
    swap = away(pair.at[0], pair.at[1], pairs, pairr, other)
    swap.start()
    if NI > 1:
        drain(rewards.at[pl.ds(0, NI - 1)], rr)
    rewards[i] = reward[...]
    mean = jnp.sum(rewards[...], axis=0) / NI
    square = jnp.sum(rewards[...] * rewards[...], axis=0) / NI
    deviates = jnp.sqrt(jnp.maximum(square - mean * mean, 0.0))
    advantage = (reward[...] - mean) / jnp.maximum(deviates, 1.0)
    swap.wait()
    ratio_now = jnp.exp((pair[0] + pair[1]) / (2 * S * HALF * C))
    clipped = jnp.clip(ratio_now, 0.8, 1.2)
    keep = ratio_now * advantage <= clipped * advantage
    gain = jnp.where(keep, -ratio_now * advantage, 0.0)
    ratio[...] = ratio_now
    f = (gain * (step * branch_share))[0:1, :]
    fscale = f * D ** (-0.5)

    def paired(p):
        base = 2 * p * n3
        a, b = gv[base : base + n3], gv[base + n3 : base + 2 * n3]
        return (jnp.where(iota(a.shape, 1) < C, a, b) * f).reshape(S, third, D)

    def text_values(p):
        v = gv[NKI + p * H * TXT : NKI + (p + 1) * H * TXT]
        v = (jnp.where(iota(v.shape, 1) < C, v, 0.0) * f).reshape(H, TXT, D)
        return jnp.concatenate([jnp.zeros_like(v), v], axis=1)

    uo[...] = paired(1).astype(BF16)
    uto[...] = text_values(1).astype(BF16)
    swaps = [
        away(uo, xu, xs.at[0], xr.at[0], other),
        away(uto, xut, xs.at[1], xr.at[1], other),
        away(ko, xk, xs.at[2], xr.at[2], other),
        away(kto, xkt, xs.at[3], xr.at[3], other),
    ]
    swaps[0].start()
    swaps[1].start()
    cols_home = pl.ds(pl.multiple_of(head * D, D), D)
    mine = pl.ds(pl.multiple_of(HALF * c, HALF), HALF)

    def send_narrow():
        swaps[0].wait_recv()
        uf[...] = (paired(0) + xu[...].astype(F32)).astype(BF16)
        swaps[1].wait_recv()
        utf[...] = (text_values(0) + xut[...].astype(F32)).astype(BF16)

        def one(k, carry):
            t = at_distance(k // YN, 1) * YN + lax.rem(y + k, YN)
            put(uf.at[t], ub.at[head, c], us, ur, branch, t)
            return carry

        lax.fori_loop(0, S, one, 0)

        def one_text(k, carry):
            put(utf.at[k], utb.at[head], uts, utr, branch, c * H + k)
            return carry

        lax.fori_loop(0, H, one_text, 0)

    def widen_all():
        drain(ub, ur)
        drain(utb, utr)

        def widen(h, carry):
            at = pl.ds(pl.multiple_of(h * D, D), D)
            r = rt[:, at]
            twice = jnp.concatenate([r, r], axis=0)
            low = iota((third, D), 1) < C
            u0, u1 = ub[h, 0].astype(F32), ub[h, 1].astype(F32)
            spaced = jnp.concatenate(
                [
                    jnp.where(low, u0, 0.0),
                    jnp.where(low, 0.0, u0),
                    jnp.where(low, u1, 0.0),
                    jnp.where(low, 0.0, u1),
                    utb[h].astype(F32),
                ],
                axis=0,
            )
            wide = jnp.dot(spaced.astype(BF16), twice, preferred_element_type=F32)
            dv[:, at] = wide[: 2 * HALF].astype(BF16)
            tgrad[:, at] = wide[2 * HALF :].astype(BF16)
            values = jnp.concatenate([vbuf[:, at], tx[:, at]], axis=0)
            res = jnp.dot(spaced.T.astype(BF16), values, preferred_element_type=F32)
            rgp[:, at] = res[:C] + res[C:]
            return carry

        lax.fori_loop(0, H, widen, 0)
        pltpu.make_async_copy(dv, grad.at[2], dvsem).start()

    def peers():
        for k in range(1, NP):
            p = lax.rem(me + k, NP)
            yield p, {"cfg": lax.rem(p, 2), "img": p // 2}

    def piece(p):
        return pl.ds(pl.multiple_of(p * W, D), W)

    def strip(n):
        return pl.ds(pl.multiple_of(n * RY, 8), RY)

    def readout_1():
        for p, device in peers():
            away(rgp.at[:, piece(p)], r1.at[me], as_.at[0], ar.at[0], device).start()

    def readout_2():
        drain(r1.at[pl.ds(0, NP - 1)], ar.at[0])
        r1[me] = rgp[:, piece(me)]
        a1[...] = jnp.sum(r1[...], axis=0)
        for k in range(1, YN):
            n = lax.rem(y + k, YN)
            away(a1.at[strip(n)], r2.at[y], as_.at[1], ar.at[1], {"seq": z * YN + n}).start()

    def readout_3():
        drain(r2.at[pl.ds(0, YN - 1)], ar.at[1])
        r2[y] = a1[strip(y), :]
        a2[...] = jnp.sum(r2[...], axis=0)
        for k in range(1, ZN):
            n = lax.rem(z + k, ZN)
            away(a2, r3.at[z], as_.at[2], ar.at[2], {"seq": n * YN + y}).start()

    def readout_4():
        if ZN > 1:
            drain(r3.at[pl.ds(0, ZN - 1)], ar.at[2])
        r3[z] = a2[...]
        a3[...] = jnp.sum(r3[...], axis=0)
        for k in range(1, YN):
            n = lax.rem(y + k, YN)
            away(a3, r4.at[y], as_.at[3], ar.at[3], {"seq": z * YN + n}).start()

    def readout_5():
        drain(r4.at[pl.ds(0, YN - 1)], ar.at[3])
        r4[y] = a3[...]
        pltpu.make_async_copy(r4, rg.at[:, :, piece(me)], ls).start()
        for p, device in peers():
            away(r4, rg.at[:, :, piece(me)], as_.at[4], ar.at[4], device).start()

    steps = dict(
        send_narrow=send_narrow, widen_all=widen_all, readout_1=readout_1, readout_2=readout_2,
        readout_3=readout_3, readout_4=readout_4, readout_5=readout_5,
    )

    def key_grads(n, carry):
        zs = at_distance(n, -1)
        block = qbuf[pl.ds(zs * YN, YN)].reshape(QB, D)
        g_t = gl[zs]
        shift = delta[zs]

        def one(rows, dq_t):
            gp = jnp.dot(narrow[rows], g_t, preferred_element_type=F32)
            ds = (weights[zs, rows].astype(F32) * (gp - shift)).astype(BF16)
            gk[rows] += jnp.dot(ds, block, preferred_element_type=F32)
            return dq_t + jnp.dot(keys_t[:, rows], ds, preferred_element_type=F32)

        dq_t = over_keys(one, jnp.zeros((D, QB), F32))
        dqb[pl.ds(zs * YN, YN)] = (dq_t.T * fscale).astype(BF16).reshape(YN, HALF, D)
        for yy in range(YN):
            t = zs * YN + yy
            put(dqb.at[t], grad.at[0, mine, cols_home], dqs, dqr, branch, t)
        for at, what in EVENTS:
            pl.when(n == min(at, ZN - 1))(steps[what])
        return carry

    lax.fori_loop(0, ZN, key_grads, 0)

    def image_keys(p):
        base = 2 * p * n3
        a = gk[base : base + n3].reshape(S, third, D)
        b = gk[base + n3 : base + 2 * n3].reshape(S, third, D)
        return jnp.concatenate([a, b], axis=1) * fscale

    def text_keys(p):
        k = gk[NKI + p * H * TXT : NKI + (p + 1) * H * TXT]
        k = (k * fscale).reshape(H, TXT, D)
        return jnp.concatenate([k, jnp.zeros_like(k)], axis=1)

    ko[...] = image_keys(1).astype(BF16)
    swaps[2].start()
    kto[...] = text_keys(1).astype(BF16)
    swaps[3].start()
    swaps[2].wait_recv()
    kf[...] = (image_keys(0) + xk[...].astype(F32)).astype(BF16)

    def send_key_grads(k, carry):
        t = at_distance(k // YN, 1) * YN + lax.rem(y + k, YN)
        put(kf.at[t], grad.at[1, mine, cols_home], dks, dkr, branch, t)
        return carry

    lax.fori_loop(0, S, send_key_grads, 0)
    swaps[3].wait_recv()
    ktf[...] = (text_keys(0) + xkt[...].astype(F32)).astype(BF16)

    def send_text_keys(k, carry):
        put(ktf.at[k], ktb.at[head], kts, ktr, branch, c * H + k)
        return carry

    lax.fori_loop(0, H, send_text_keys, 0)

    def sent(k, carry):
        chip = 2 * k + c
        for odd in range(2):
            src = 2 * k + odd
            drain(kv.at[1, src], fs.at[src])
        drain(text.at[1, k], fts.at[k])
        for j in range(2):
            @pl.when(jnp.logical_not(jnp.logical_and(chip == s, j == c)))
            def _():
                drain(kv.at[0, 0], ks.at[k, j])
                drain(qbuf.at[0], qs.at[k, j])

        @pl.when(jnp.logical_not(jnp.logical_and(chip == s, side == c)))
        def _():
            drain(text.at[0, 0], ts.at[k])

        return carry

    lax.fori_loop(0, H, sent, 0)
    drain(got.at[pl.ds(0, S - 1)], ms)
    drain(g_all.at[pl.ds(0, S - 1)], gs)
    drain(parts.at[pl.ds(0, S - 1)], ps)
    if NI > 1:
        drain(rewards.at[pl.ds(0, NI - 1)], rs)
    for w in swaps:
        w.wait_send()
    drain(r1.at[pl.ds(0, NP - 1)], as_.at[0])
    drain(r2.at[pl.ds(0, YN - 1)], as_.at[1])
    if ZN > 1:
        drain(r3.at[pl.ds(0, ZN - 1)], as_.at[2])
    drain(r4.at[pl.ds(0, YN - 1)], as_.at[3])
    drain(r1.at[pl.ds(0, NP - 1)], as_.at[4])
    drain(r4, ls)
    drain(r1.at[pl.ds(0, NP - 1)], ar.at[4])
    drain(dv, dvsem)
    text_here = jnp.logical_and(branch == c, s // H == c)

    @pl.when(branch == c)
    def _():
        drain(uf.at[pl.ds(0, S - 1)], us)
        drain(dqb.at[pl.ds(0, S - 1)], dqs)
        drain(kf.at[pl.ds(0, S - 1)], dks)

    @pl.when(branch != c)
    def _():
        drain(uf, us)
        drain(dqb, dqs)
        drain(kf, dks)

    @pl.when(text_here)
    def _():
        drain(utf.at[pl.ds(0, H - 1)], uts)
        drain(ktf.at[pl.ds(0, H - 1)], kts)

    @pl.when(jnp.logical_not(text_here))
    def _():
        drain(utf, uts)
        drain(ktf, kts)

    drain(ktb, ktr)

    def text_home(h, carry):
        at = pl.ds(pl.multiple_of(h * D, D), D)
        t = ktb[h].astype(F32)
        tgrad[:, at] = jnp.where(iota(t.shape, 0) < TXT, t, tgrad[:, at].astype(F32)).astype(BF16)
        return carry

    lax.fori_loop(0, H, text_home, 0)
    drain(grad.at[0], dqr)
    drain(grad.at[1], dkr)


EVENTS = (
    (0, "send_narrow"),
    (2, "widen_all"),
    (2, "readout_1"),
    (3, "readout_2"),
    (4, "readout_3"),
    (5, "readout_4"),
    (6, "readout_5"),
)


def step_call(S, NI, guidance, rate, img, tx, rt, noise, old, reward):
    H, ZN, NP = S // 2, S // YN, 2 * NI
    HD = rt.shape[1]
    W, RY, third = HD // NP, C // YN, HALF // 2
    NK = (2 * HALF + TXT) * S
    dma = pltpu.SemaphoreType.DMA
    tile = (8, D)
    b = lambda *shape: pltpu.VMEM(shape, BF16)
    w = lambda *shape: pltpu.VMEM(shape, F32)
    return pl.pallas_call(
        functools.partial(step_kernel, S, NI),
        out_shape=(
            jax.ShapeDtypeStruct(img.shape, BF16),
            jax.ShapeDtypeStruct((2 * TXT, HD), BF16),
            jax.ShapeDtypeStruct((YN, RY, HD), F32),
            jax.ShapeDtypeStruct(tile, F32),
        ),
        in_specs=[SMEM, SMEM, ANY, VMEM, VMEM, VMEM, VMEM, VMEM],
        out_specs=(ANY, VMEM, ANY, VMEM),
        scratch_shapes=[
            b(*img.shape[1:]),
            b(H, 2, third, D),
            b(H, 2 * TXT, D),
            b(2, S, HALF + third, D),
            b(2, H, 2 * TXT, D),
            b(S, HALF, D),
            b(NK, 2 * D),
            b(D, NK),
            b(NK, D),
            b(C + ONES, NK),
            w(NK, QB),
            w(NK, QB),
            *([b(SB, QB)] * 4),
            b(TXT * S, QB),
            b(ZN, NK, QB),
            w(ZN, C, QB),
            w(ZN, 1, QB),
            b(S, C // 2, D),
            b(S, C // 2, D),
            b(C // 2, D),
            b(S, C // 2, D),
            w(*tile),
            w(S, *tile),
            w(2, *tile),
            w(NI, *tile),
            b(ZN, 2 * C, QB),
            w(ZN, 1, QB),
            w(NK, D),
            w(NK, D),
            b(S, third, D),
            b(S, third, D),
            b(S, third, D),
            b(H, 2 * TXT, D),
            b(H, 2 * TXT, D),
            b(H, 2 * TXT, D),
            b(S, HALF, D),
            b(S, HALF, D),
            b(S, HALF, D),
            b(H, 2 * TXT, D),
            b(H, 2 * TXT, D),
            b(H, 2 * TXT, D),
            b(S, HALF, D),
            b(H, 2, third, D),
            b(H, 2 * TXT, D),
            b(H, 2 * TXT, D),
            b(*img.shape[1:]),
            w(C, HD),
            w(NP, C, W),
            w(C, W),
            w(YN, RY, W),
            w(RY, W),
            w(ZN, RY, W),
            w(RY, W),
            w(YN, RY, W),
            dma,
            dma((H, 2)), dma((S,)),
            dma((H, 2)), dma((S,)),
            dma((H,)), dma((H,)),
            dma((S,)), dma((S,)),
            dma((H,)), dma((H,)),
            dma, dma,
            dma, dma((S,)),
            dma, dma,
            dma, dma,
            dma, dma,
            dma((4,)), dma((4,)),
            dma, dma,
            dma, dma,
            dma, dma,
            dma, dma,
            dma, dma,
            dma,
            dma((5,)), dma((5,)),
            dma,
        ],
        compiler_params=pltpu.CompilerParams(
            collective_id=0, has_side_effects=True, vmem_limit_bytes=LIMIT
        ),
        name="step",
    )(guidance, rate, img, tx, rt, noise, old, reward)


def on_device(S, NI, img_qkv, txt_kv, readout, old_velocity, noise, step_ratio, rewards, guidance):
    img = img_qkv[0, 0].transpose(1, 0, 2)
    text = txt_kv[0, 0]
    tx = jnp.concatenate([text[:, 0], text[:, 1]], axis=0)
    scalar = lambda x: x.reshape(1, 1)
    reward = jnp.broadcast_to(scalar(rewards), (8, D))
    grad, tgrad, rg, ratio = step_call(
        S, NI, scalar(guidance), scalar(step_ratio), img, tx, readout.T, noise[0].T, old_velocity[0].T, reward
    )
    img_grad = grad.transpose(1, 0, 2)[None, None]
    txt_grad = jnp.stack([tgrad[:TXT], tgrad[TXT:]], axis=1)[None, None]
    return (img_grad, txt_grad, rg.reshape(C, -1).T, ratio[0, :1])


def solution(mesh):
    S, NI = mesh.shape["seq"], mesh.shape["img"]
    placed = (
        P("cfg", "img", "seq", None, None),
        P("cfg", "img", "seq", None, None),
        P(),
        P("img", "seq", None),
        P("img", "seq", None),
        P("img"),
        P("img"),
        P(),
    )
    return jax.shard_map(
        functools.partial(on_device, S, NI),
        mesh=mesh,
        in_specs=placed,
        out_specs=(
            P("cfg", "img", "seq", None, None),
            P("cfg", "img", "seq", None, None),
            P(),
            P("img"),
        ),
        check_vma=False,
    )
```

time: 420 us -> 159 us (0.38); the launches traced: 412 us -> 156 us
  Pallas kernels: 0 us -> 145 us
  waiting for transfers between devices: 108 us -> 0 us
  matrix products: 72.3 us -> 0 us
  blocking collectives: 69.8 us -> 0 us
  other arithmetic: 65.8 us -> 0.64 us
  starting transfers between devices: 52.2 us -> 0 us
  local copies, waits for them, and re-layouts: 36 us -> 7.72 us
  between operations: 7.66 us -> 2.59 us
    pallas_call x0 -> x1, Pallas kernels: none -> 145 us  [step_call(): pl.pallas_call(functools.partial(step_kernel, S, NI), out_shape=(jax.Shap...]
    dot_general x27 -> x0, matrix products: 72.3 us -> none  [the longest x4 19.7 us: one_block(): jnp.einsum('hqk,qhd->khd', prob, grad_block, preferred_element_type=jnp.f...]
    all_to_all x3 -> x0, blocking collectives: 69.8 us -> none  [the longest x1 42.2 us: side_by_side(): lax.all_to_all(both, axis, split_axis=split_dim, concat_axis=concat_dim,...]
    all_to_all x8 -> x0, waiting for transfers between devices: 68 us -> none  [the longest x1 29.8 us: side_by_side(): lax.all_to_all(both, axis, split_axis=split_dim, concat_axis=concat_dim,...]
    all_to_all x8 -> x0, starting transfers between devices: 45.1 us -> none  [the longest x4 20.7 us: from_everyone(): return lax.all_to_all(copies, axis, split_axis=0, concat_axis=0, tiled=True)]
    ppermute x5 -> x0, waiting for transfers between devices: 40.1 us -> none  [swapped(): return lax.ppermute(block, axis, route)]
    convert_element_type x6 -> x0, other arithmetic: 27.8 us -> none  [the longest x4 26.3 us: one_block(): grad_scores = (weights * (grad_probs - delta) * scale).astype(jnp.bfloat16)]
    dynamic_update_slice x4 -> x0, other arithmetic: 14.9 us -> none  [attend_forward(): probs, mixed = lax.map(one_block, query_blocks)]
  transfers between devices with their start and end apart: 13 -> 0, of which waited for: 9 -> 0; matrix products, arithmetic and copies ran while one was open for 35% -> 0% of each run, Pallas kernels for 0% -> 0%
where the time goes in v2:
time: 159 us; the launch traced here: 156 us
  Pallas kernels  145 us (91%)
  local copies, waits for them, and re-layouts  7.72 us (5%)
  between operations  2.59 us (2%)
    pallas_call x1, Pallas kernels, step_call(): pl.pallas_call(functools.partial(step_kernel, S, NI), out_shape=(jax.Shap...  145 us
    unnamed x6, local copies, waits for them, and re-layouts  5.14 us

profile of v2, /device:TPU:5, one launch (start us, length us, event | category | flops | bytes accessed | tf_op | source)
XLA Modules:
  0.0 156.4 jit_solution(7883573798115274271)
XLA Ops:
  2.6 0.6 broadcast_in_dim.14.reward
  3.2 0.9 copy.15
  4.0 0.6 pad_maximum_fusion.tx
  4.7 145.4 %step.1 = (bf16[3,128,2048]{2,1,0:T(8,128)(2,1)}, bf16[16,2048]{1,0:T(8,128)(2,1)}, f32[4,16,2048]{2,1,0:T(8,128)}, f32[8,128]{1,0:T(8,128)}) custom-call(f32[1,1]{1,0:T(1,128)} %bitcast.35.guidance, f32[1,1]{1,0:T(1,128)} %bitcast.33.rate, bf16[3,128,2048]{2,1,0:T(8,128)(2,1)} %bitcast.36, bf16[16,2048]{1,0:T(8,128)(2,1)} %pad_maximum_fusion.tx, ...), custom_call_target="tpu_custom_call" | custom-call | tf_op jit(solution)/shard_map/step/pallas_call | solution.py:680
  150.1 1.2 slice.19
  151.3 0.8 slice_bitcast_fusion.3
  152.1 0.7 copy.13
  152.8 0.0 copy-start
  152.8 2.8 %copy.21 = bf16[1,1,128,3,2048]{4,2,3,1,0:T(8,128)(2,1)} copy(bf16[1,1,128,3,2048]{4,2,3,1,0:T(8,128)(2,1)} %bitcast.37) | data formatting | bytes 3145728
  155.6 0.0 copy-done
  155.6 0.8 copy.22
  (2 shorter events, 0.0 us)
Async XLA Ops:
  152.8 2.8 %copy-start = (f32[4,16,2048]{2,1,0:T(8,128)S(1)}, f32[4,16,2048]{2,1,0:T(8,128)}, u32[]{:S(2)}) copy-start(f32[4,16,2048]{2,1,0:T(8,128)} %get-tuple-element.10) | copy-start | bytes 1572868

commit v3 on v2

--- a/solution.py
+++ b/solution.py
@@ -58,21 +58,25 @@
     pltpu.make_async_copy(ref, ref, sem).wait()
 
 
+def wrap(at, size):
+    return jnp.where(at >= size, at - size, at)
+
+
 def signal_plane(chips):
     c, s = lax.axis_index("cfg"), lax.axis_index("seq")
     barrier = pltpu.get_barrier_semaphore()
 
+    def tell(device):
+        pl.semaphore_signal(barrier, inc=1, device_id=device, device_id_type=MESH)
+
     def one(k, carry):
-        n = lax.rem(c * chips + s + k, 2 * chips)
-        pl.semaphore_signal(
-            barrier,
-            inc=1,
-            device_id={"cfg": n // chips, "seq": lax.rem(n, chips)},
-            device_id_type=MESH,
-        )
-        return carry
-
-    lax.fori_loop(1, 2 * chips, one, 0)
+        chip = wrap(s + k, chips)
+        tell({"cfg": c, "seq": chip})
+        tell({"cfg": 1 - c, "seq": chip})
+        return carry
+
+    lax.fori_loop(1, chips, one, 0)
+    tell({"cfg": 1 - c})
     return barrier
 
 
@@ -98,13 +102,13 @@
 
 
 def step_kernel(
-    S, NI, guidance, rate, img, tx, rt, noise, old, reward,
+    S, NI, guidance, rate, reward, img, tx, rt, noise, old,
     grad, tgrad, rg, ratio,
     vbuf, vrp, txb, kv, text, qbuf, keys, keys_t, narrow, narrow_t, scores_a, scores_b, hold_0, hold_1, hold_2, hold_3, hold_text, weights, out_t, linv,
-    msg, got, g_own, g_all, part, parts, pair, rewards, gl, delta, gk, gv,
-    uo, xu, uf, uto, xut, utf, ko, xk, kf, kto, xkt, ktf, dqb, ub, utb, ktb, dv, rgp, r1, a1, r2, a2, r3, a3, r4,
+    msg, got, g_own, g_all, part, parts, pair, rewards, reward_own, gl, gl_cols, delta, gk,
+    uo, xu, uown, uf, uto, xut, utf, ko, xk, kf, kto, xkt, ktf, dqb, ub, utb, ktb, dv, rgp, rx, rh, rhb, r1, a1, r2, a2, r3, a3, r4,
     vsem, ks, kr, qs, qr, ts, tr, fs, fr, fts, ftr, ms, mr, gs, gr, ps, pr, pairs, pairr, rs, rr,
-    xs, xr, us, ur, uts, utr, dqs, dqr, dks, dkr, kts, ktr, dvsem, as_, ar, ls,
+    xs, xr, xus, xur, us, ur, uts, utr, dqs, dqr, dks, dkr, kts, ktr, dvsem, as_, ar, ls,
 ):
     H = S // 2
     ZN = S // YN
@@ -119,7 +123,6 @@
     c, i, s = lax.axis_index("cfg"), lax.axis_index("img"), lax.axis_index("seq")
     head, branch = s // 2, lax.rem(s, 2)
     y, z = lax.rem(s, YN), s // YN
-    me = 2 * i + c
     other = {"cfg": 1 - c}
 
     vcopy = pltpu.make_async_copy(img.at[2], vbuf, vsem)
@@ -128,11 +131,12 @@
     for k in range(1, NI):
         for core in range(2):
             pl.semaphore_signal(
-                barrier, inc=1, device_id={"cfg": core, "img": lax.rem(i + k, NI)}, device_id_type=MESH
+                barrier, inc=1, device_id={"cfg": core, "img": wrap(i + k, NI)}, device_id_type=MESH
             )
     vcopy.wait()
-
-    def squeeze(h, carry):
+    reward_own[...] = jnp.full(reward_own.shape, reward[0, 0], F32)
+
+    def squeeze(h):
         cols = pl.ds(pl.multiple_of(h * D, D), D)
         r = rt[:, cols]
         twice = jnp.concatenate([r, r], axis=0)
@@ -146,16 +150,31 @@
         yv = lax.dot_general(t, twice, NT, preferred_element_type=F32)
         yv = jnp.where(iota(yv.shape, 1) < C, yv, 0.0)
         txb[h] = jnp.where(iota(yv.shape, 0) < TXT, t.astype(F32), yv).astype(BF16)
-        return carry
-
-    lax.fori_loop(0, H, squeeze, 0)
+
+    def some(count, body):
+        at_once = 4 if count % 4 == 0 else 1
+
+        def trip(k, carry):
+            for j in range(at_once):
+                body(k * at_once + j)
+            return carry
+
+        lax.fori_loop(0, count // at_once, trip, 0)
+
+    some(H, squeeze)
     pl.semaphore_wait(barrier, 2 * S - 1 + 2 * (NI - 1))
 
     side = s // H
 
     def at_distance(n, sign):
-        far = (n + 1) // 2
-        return lax.rem(z + jnp.where(lax.rem(n, 2) == 1, sign * far, -sign * far) + ZN, ZN)
+        half = (n + 1) // 2
+        far = jnp.where(n == 2 * half, ZN - half, half)
+        return wrap(z + far, ZN) if sign > 0 else wrap(z + ZN - far, ZN)
+
+    def in_turn(n, sign):
+        if ZN < 4:
+            return at_distance(n, sign)
+        return at_distance(jnp.where(n == 0, 0, jnp.where(n <= ZN - 3, n + 2, n - (ZN - 3))), sign)
 
     def send_keys(k, carry):
         zt = at_distance(k // 2, 1)
@@ -171,7 +190,7 @@
     lax.fori_loop(0, H, send_keys, 0)
 
     def send_queries(k, carry):
-        zt = at_distance(k // 2, 1)
+        zt = in_turn(k // 2, 1)
         h = 2 * zt + lax.rem(k, 2)
         chip = 2 * h + c
         cols = pl.ds(pl.multiple_of(h * D, D), D)
@@ -181,7 +200,7 @@
 
     lax.fori_loop(0, H, send_queries, 0)
     for k in range(1, NI):
-        away(reward, rewards.at[i], rs, rr, {"img": lax.rem(i + k, NI)}).start()
+        away(reward_own, rewards.at[i], rs, rr, {"img": wrap(i + k, NI)}).start()
 
     narrow_t[C:] = jnp.where(iota((ONES, NK), 0) == 0, 1.0, 0.0).astype(BF16)
 
@@ -285,9 +304,9 @@
         return score(scores_a, last, q_t, lax.fori_loop(0, parts_of, body, low_top))
 
     def attend(n, now, then, top8, ahead):
-        zs = at_distance(n, -1)
+        zs = in_turn(n, -1)
         top = jnp.max(top8, axis=0, keepdims=True)
-        q_t = queries_t(at_distance(n + 1, -1)) if ahead else None
+        q_t = queries_t(in_turn(n + 1, -1)) if ahead else None
         next8 = score(then, last, q_t, low_top) if ahead else low_top
         weigh(now, zs, last, top, hold_text)
         mixed = mix(last, hold_text, no_mix)
@@ -318,7 +337,7 @@
             put(msg.at[t], got.at[s], ms, mr, c, t)
         return next8
 
-    top = first_scores(queries_t(at_distance(0, -1)))
+    top = first_scores(queries_t(in_turn(0, -1)))
 
     def two(m, top):
         top = attend(2 * m, scores_a, scores_b, top, True)
@@ -340,27 +359,25 @@
     g_own[...] = (noise_own - deviation).astype(BF16)
 
     def share(k, carry):
-        t = at_distance(k // YN, 1) * YN + lax.rem(y + k, YN)
-        put(g_own, g_all.at[s], gs, gr.at[s], c, t)
-        return carry
-
-    lax.fori_loop(0, S, share, 0)
+        zt = at_distance(k, 1)
+        for yy in range(YN):
+            put(g_own, g_all.at[s], gs, gr, c, zt * YN + yy)
+        return carry
+
+    lax.fori_loop(0, ZN, share, 0)
     partial = jnp.sum(noise_own * deviation - 0.5 * deviation * deviation)
     part[...] = jnp.full(part.shape, partial, F32)
 
     def tell(k, carry):
-        put(part, parts.at[s], ps, pr, c, lax.rem(s + k, S))
+        put(part, parts.at[s], ps, pr, c, k)
         return carry
 
     lax.fori_loop(0, S, tell, 0)
-
-    gv[...] = jnp.zeros_like(gv)
     gk[...] = jnp.zeros_like(gk)
 
-    def narrow_grads(n, carry):
-        zs = at_distance(n, -1)
-        for yy in range(YN):
-            drain(g_all.at[zs * YN + yy], gr.at[zs * YN + yy])
+    drain(g_all, gr)
+
+    def divide(zs, carry):
         g_t = jnp.concatenate(
             [
                 unpack_pair(g_all[zs * YN + 2 * m].astype(F32), g_all[zs * YN + 2 * m + 1].astype(F32))
@@ -371,18 +388,13 @@
         g_t = g_t * linv[zs]
         hi = g_t.astype(BF16)
         lo = (g_t - hi.astype(F32)).astype(BF16)
+        hi32 = hi.astype(F32)
         gl[zs] = jnp.concatenate([hi, lo], axis=0)
-        delta[zs] = jnp.sum((hi.astype(F32) + lo.astype(F32)) * out_t[zs], axis=0, keepdims=True)
-        hi32 = hi.astype(F32)
-        cols = jnp.concatenate([hi32, hi32], axis=0).T.astype(BF16)
-
-        def one(rows, cr):
-            gv[rows] += jnp.dot(weights[zs, rows], cols, preferred_element_type=F32)
-            return cr
-
-        return over_keys(one, carry)
-
-    lax.fori_loop(0, ZN, narrow_grads, 0)
+        delta[zs] = jnp.sum((hi32 + lo.astype(F32)) * out_t[zs], axis=0, keepdims=True)
+        gl_cols[zs] = jnp.concatenate([hi32, hi32], axis=0).T.astype(BF16)
+        return carry
+
+    lax.fori_loop(0, ZN, divide, 0)
 
     drain(parts, pr)
     pair[0] = jnp.sum(parts[...], axis=0)
@@ -390,67 +402,98 @@
     swap.start()
     if NI > 1:
         drain(rewards.at[pl.ds(0, NI - 1)], rr)
-    rewards[i] = reward[...]
+    own_reward = reward_own[...]
+    rewards[i] = own_reward
     mean = jnp.sum(rewards[...], axis=0) / NI
     square = jnp.sum(rewards[...] * rewards[...], axis=0) / NI
     deviates = jnp.sqrt(jnp.maximum(square - mean * mean, 0.0))
-    advantage = (reward[...] - mean) / jnp.maximum(deviates, 1.0)
+    advantage = (own_reward - mean) / jnp.maximum(deviates, 1.0)
     swap.wait()
     ratio_now = jnp.exp((pair[0] + pair[1]) / (2 * S * HALF * C))
     clipped = jnp.clip(ratio_now, 0.8, 1.2)
     keep = ratio_now * advantage <= clipped * advantage
     gain = jnp.where(keep, -ratio_now * advantage, 0.0)
-    ratio[...] = ratio_now
+    ratio[0, 0] = jnp.max(ratio_now)
     f = (gain * (step * branch_share))[0:1, :]
     fscale = f * D ** (-0.5)
 
-    def paired(p):
-        base = 2 * p * n3
-        a, b = gv[base : base + n3], gv[base + n3 : base + 2 * n3]
-        return (jnp.where(iota(a.shape, 1) < C, a, b) * f).reshape(S, third, D)
-
-    def text_values(p):
-        v = gv[NKI + p * H * TXT : NKI + (p + 1) * H * TXT]
-        v = (jnp.where(iota(v.shape, 1) < C, v, 0.0) * f).reshape(H, TXT, D)
-        return jnp.concatenate([jnp.zeros_like(v), v], axis=1)
-
-    uo[...] = paired(1).astype(BF16)
-    uto[...] = text_values(1).astype(BF16)
-    swaps = [
-        away(uo, xu, xs.at[0], xr.at[0], other),
-        away(uto, xut, xs.at[1], xr.at[1], other),
-        away(ko, xk, xs.at[2], xr.at[2], other),
-        away(kto, xkt, xs.at[3], xr.at[3], other),
-    ]
-    swaps[0].start()
-    swaps[1].start()
     cols_home = pl.ds(pl.multiple_of(head * D, D), D)
     mine = pl.ds(pl.multiple_of(HALF * c, HALF), HALF)
-
-    def send_narrow():
-        swaps[0].wait_recv()
-        uf[...] = (paired(0) + xu[...].astype(F32)).astype(BF16)
-        swaps[1].wait_recv()
-        utf[...] = (text_values(0) + xut[...].astype(F32)).astype(BF16)
+    NG = max(1, n3 // SB)
+    GS = S // NG
+    GR = third * GS
+
+    def narrow_grad(rows):
+        total = jnp.dot(weights[0, rows], gl_cols[0], preferred_element_type=F32)
+        for zs in range(1, ZN):
+            total = total + jnp.dot(weights[zs, rows], gl_cols[zs], preferred_element_type=F32)
+        return total * f
+
+    def paired(p, r):
+        a, b = (
+            narrow_grad(pl.ds(pl.multiple_of((2 * p + ab) * n3 + r * GR, GR), GR)) for ab in range(2)
+        )
+        return jnp.where(iota(a.shape, 1) < C, a, b).reshape(GS, third, D)
+
+    def swap_u(r):
+        srcs = pl.ds(r * GS, GS)
+        return away(uo.at[srcs], xu.at[srcs], xus.at[r], xur.at[r], other)
+
+    def send_u(r):
+        swap_u(r).wait_recv()
+        srcs = pl.ds(r * GS, GS)
+        uf[srcs] = (uown[srcs] + xu[srcs].astype(F32)).astype(BF16)
 
         def one(k, carry):
-            t = at_distance(k // YN, 1) * YN + lax.rem(y + k, YN)
+            t = r * GS + k
             put(uf.at[t], ub.at[head, c], us, ur, branch, t)
             return carry
 
-        lax.fori_loop(0, S, one, 0)
-
-        def one_text(k, carry):
-            put(utf.at[k], utb.at[head], uts, utr, branch, c * H + k)
-            return carry
-
-        lax.fori_loop(0, H, one_text, 0)
+        lax.fori_loop(0, GS, one, 0)
+
+    def group(k):
+        return wrap(z * NG // ZN + k, NG)
+
+    swaps = [
+        away(uto, xut, xs.at[0], xr.at[0], other),
+        away(ko, xk, xs.at[1], xr.at[1], other),
+        away(kto, xkt, xs.at[2], xr.at[2], other),
+    ]
+    both_texts = narrow_grad(last)
+    both_texts = jnp.where(iota(both_texts.shape, 1) < C, both_texts, 0.0).reshape(2, H, TXT, D)
+    no_keys = jnp.zeros((H, TXT, D), F32)
+    uto[...] = jnp.concatenate([no_keys, both_texts[1]], axis=1).astype(BF16)
+    swaps[0].start()
+
+    def narrow_group(k, carry):
+        r = group(k)
+        srcs = pl.ds(r * GS, GS)
+        uo[srcs] = paired(1, r).astype(BF16)
+        swap_u(r).start()
+        uown[srcs] = paired(0, r)
+
+        @pl.when(k > 0)
+        def _():
+            send_u(group(k - 1))
+
+        return carry
+
+    lax.fori_loop(0, NG, narrow_group, 0)
+    swaps[0].wait_recv()
+    utf[...] = (jnp.concatenate([no_keys, both_texts[0]], axis=1) + xut[...].astype(F32)).astype(BF16)
+
+    def send_text(k, carry):
+        put(utf.at[k], utb.at[head], uts, utr, branch, c * H + k)
+        return carry
+
+    lax.fori_loop(0, H, send_text, 0)
+    send_u(group(NG - 1))
 
     def widen_all():
         drain(ub, ur)
         drain(utb, utr)
 
-        def widen(h, carry):
+        def widen(h):
             at = pl.ds(pl.multiple_of(h * D, D), D)
             r = rt[:, at]
             twice = jnp.concatenate([r, r], axis=0)
@@ -472,61 +515,71 @@
             values = jnp.concatenate([vbuf[:, at], tx[:, at]], axis=0)
             res = jnp.dot(spaced.T.astype(BF16), values, preferred_element_type=F32)
             rgp[:, at] = res[:C] + res[C:]
-            return carry
-
-        lax.fori_loop(0, H, widen, 0)
+
+        some(H, widen)
         pltpu.make_async_copy(dv, grad.at[2], dvsem).start()
 
-    def peers():
-        for k in range(1, NP):
-            p = lax.rem(me + k, NP)
-            yield p, {"cfg": lax.rem(p, 2), "img": p // 2}
-
-    def piece(p):
-        return pl.ds(pl.multiple_of(p * W, D), W)
+    HW = NI * W
+
+    def half(core):
+        return pl.ds(pl.multiple_of(core * HW, D), HW)
+
+    def piece(n):
+        return pl.ds(pl.multiple_of(n * W, D), W)
 
     def strip(n):
         return pl.ds(pl.multiple_of(n * RY, 8), RY)
 
     def readout_1():
-        for p, device in peers():
-            away(rgp.at[:, piece(p)], r1.at[me], as_.at[0], ar.at[0], device).start()
+        away(rgp.at[:, half(1 - c)], rx, as_.at[0], ar.at[0], other).start()
 
     def readout_2():
-        drain(r1.at[pl.ds(0, NP - 1)], ar.at[0])
-        r1[me] = rgp[:, piece(me)]
-        a1[...] = jnp.sum(r1[...], axis=0)
+        drain(rx, ar.at[0])
+        rh[...] = rgp[:, half(c)] + rx[...]
+        rhb[...] = rh[...].astype(BF16)
+        for k in range(1, NI):
+            n = wrap(i + k, NI)
+            away(rhb.at[:, piece(n)], r1.at[i], as_.at[5], ar.at[5], {"img": n}).start()
+
+    def readout_3():
+        if NI > 1:
+            drain(r1.at[pl.ds(0, NI - 1)], ar.at[5])
+        r1[i] = jnp.zeros((C, W), BF16)
+        a1[...] = jnp.sum(r1[...].astype(F32), axis=0) + rh[:, piece(i)]
         for k in range(1, YN):
-            n = lax.rem(y + k, YN)
+            n = wrap(y + k, YN)
             away(a1.at[strip(n)], r2.at[y], as_.at[1], ar.at[1], {"seq": z * YN + n}).start()
 
-    def readout_3():
+    def readout_4():
         drain(r2.at[pl.ds(0, YN - 1)], ar.at[1])
         r2[y] = a1[strip(y), :]
         a2[...] = jnp.sum(r2[...], axis=0)
         for k in range(1, ZN):
-            n = lax.rem(z + k, ZN)
+            n = wrap(z + k, ZN)
             away(a2, r3.at[z], as_.at[2], ar.at[2], {"seq": n * YN + y}).start()
 
-    def readout_4():
+    def readout_5():
         if ZN > 1:
             drain(r3.at[pl.ds(0, ZN - 1)], ar.at[2])
         r3[z] = a2[...]
         a3[...] = jnp.sum(r3[...], axis=0)
         for k in range(1, YN):
-            n = lax.rem(y + k, YN)
+            n = wrap(y + k, YN)
             away(a3, r4.at[y], as_.at[3], ar.at[3], {"seq": z * YN + n}).start()
 
-    def readout_5():
+    def readout_6():
         drain(r4.at[pl.ds(0, YN - 1)], ar.at[3])
         r4[y] = a3[...]
-        pltpu.make_async_copy(r4, rg.at[:, :, piece(me)], ls).start()
-        for p, device in peers():
-            away(r4, rg.at[:, :, piece(me)], as_.at[4], ar.at[4], device).start()
+        to = rg.at[:, :, pl.ds(pl.multiple_of(c * HW + i * W, D), W)]
+        pltpu.make_async_copy(r4, to, ls).start()
+        for k in range(NI):
+            n = wrap(i + k, NI)
+            for core in (c, 1 - c) if k else (1 - c,):
+                away(r4, to, as_.at[4], ar.at[4], {"cfg": core, "img": n}).start()
 
     steps = dict(
-        send_narrow=send_narrow, widen_all=widen_all, readout_1=readout_1, readout_2=readout_2,
-        readout_3=readout_3, readout_4=readout_4, readout_5=readout_5,
+        widen_all=widen_all, readout_1=readout_1, readout_2=readout_2, readout_3=readout_3,
+        readout_4=readout_4, readout_5=readout_5, readout_6=readout_6,
     )
 
     def key_grads(n, carry):
@@ -564,19 +617,21 @@
         return jnp.concatenate([k, jnp.zeros_like(k)], axis=1)
 
     ko[...] = image_keys(1).astype(BF16)
+    swaps[1].start()
+    kto[...] = text_keys(1).astype(BF16)
     swaps[2].start()
-    kto[...] = text_keys(1).astype(BF16)
-    swaps[3].start()
+    swaps[1].wait_recv()
+    kf[...] = (image_keys(0) + xk[...].astype(F32)).astype(BF16)
+
+    def send_key_grads(k, carry):
+        zt = at_distance(k, 1)
+        for yy in range(YN):
+            t = zt * YN + yy
+            put(kf.at[t], grad.at[1, mine, cols_home], dks, dkr, branch, t)
+        return carry
+
+    lax.fori_loop(0, ZN, send_key_grads, 0)
     swaps[2].wait_recv()
-    kf[...] = (image_keys(0) + xk[...].astype(F32)).astype(BF16)
-
-    def send_key_grads(k, carry):
-        t = at_distance(k // YN, 1) * YN + lax.rem(y + k, YN)
-        put(kf.at[t], grad.at[1, mine, cols_home], dks, dkr, branch, t)
-        return carry
-
-    lax.fori_loop(0, S, send_key_grads, 0)
-    swaps[3].wait_recv()
     ktf[...] = (text_keys(0) + xkt[...].astype(F32)).astype(BF16)
 
     def send_text_keys(k, carry):
@@ -584,6 +639,8 @@
         return carry
 
     lax.fori_loop(0, H, send_text_keys, 0)
+
+    readout_6()
 
     def sent(k, carry):
         chip = 2 * k + c
@@ -611,14 +668,22 @@
         drain(rewards.at[pl.ds(0, NI - 1)], rs)
     for w in swaps:
         w.wait_send()
-    drain(r1.at[pl.ds(0, NP - 1)], as_.at[0])
+    drain(rx, as_.at[0])
+    if NI > 1:
+        drain(r1.at[pl.ds(0, NI - 1)], as_.at[5])
     drain(r2.at[pl.ds(0, YN - 1)], as_.at[1])
     if ZN > 1:
         drain(r3.at[pl.ds(0, ZN - 1)], as_.at[2])
     drain(r4.at[pl.ds(0, YN - 1)], as_.at[3])
-    drain(r1.at[pl.ds(0, NP - 1)], as_.at[4])
+    drain(rgp.at[:, pl.ds(0, (NP - 1) * W)], as_.at[4])
     drain(r4, ls)
-    drain(r1.at[pl.ds(0, NP - 1)], ar.at[4])
+    drain(rgp.at[:, pl.ds(0, (NP - 1) * W)], ar.at[4])
+
+    def swapped_u(r, carry):
+        swap_u(r).wait_send()
+        return carry
+
+    lax.fori_loop(0, NG, swapped_u, 0)
     drain(dv, dvsem)
     text_here = jnp.logical_and(branch == c, s // H == c)
 
@@ -658,17 +723,16 @@
 
 
 EVENTS = (
-    (0, "send_narrow"),
-    (2, "widen_all"),
-    (2, "readout_1"),
-    (3, "readout_2"),
+    (1, "widen_all"),
+    (1, "readout_1"),
+    (2, "readout_2"),
     (4, "readout_3"),
     (5, "readout_4"),
-    (6, "readout_5"),
+    (7, "readout_5"),
 )
 
 
-def step_call(S, NI, guidance, rate, img, tx, rt, noise, old, reward):
+def step_call(S, NI, guidance, rate, reward, img, tx, rt, noise, old):
     H, ZN, NP = S // 2, S // YN, 2 * NI
     HD = rt.shape[1]
     W, RY, third = HD // NP, C // YN, HALF // 2
@@ -683,10 +747,10 @@
             jax.ShapeDtypeStruct(img.shape, BF16),
             jax.ShapeDtypeStruct((2 * TXT, HD), BF16),
             jax.ShapeDtypeStruct((YN, RY, HD), F32),
-            jax.ShapeDtypeStruct(tile, F32),
+            jax.ShapeDtypeStruct((1, 1), F32),
         ),
-        in_specs=[SMEM, SMEM, ANY, VMEM, VMEM, VMEM, VMEM, VMEM],
-        out_specs=(ANY, VMEM, ANY, VMEM),
+        in_specs=[SMEM, SMEM, SMEM, ANY, VMEM, VMEM, VMEM, VMEM],
+        out_specs=(ANY, VMEM, ANY, SMEM),
         scratch_shapes=[
             b(*img.shape[1:]),
             b(H, 2, third, D),
@@ -713,12 +777,14 @@
             w(S, *tile),
             w(2, *tile),
             w(NI, *tile),
+            w(*tile),
             b(ZN, 2 * C, QB),
+            b(ZN, QB, D),
             w(ZN, 1, QB),
-            w(NK, D),
             w(NK, D),
             b(S, third, D),
             b(S, third, D),
+            w(S, third, D),
             b(S, third, D),
             b(H, 2 * TXT, D),
             b(H, 2 * TXT, D),
@@ -735,7 +801,10 @@
             b(H, 2 * TXT, D),
             b(*img.shape[1:]),
             w(C, HD),
-            w(NP, C, W),
+            w(C, NI * W),
+            w(C, NI * W),
+            b(C, NI * W),
+            b(NI, C, W),
             w(C, W),
             w(YN, RY, W),
             w(RY, W),
@@ -749,25 +818,26 @@
             dma((S,)), dma((S,)),
             dma((H,)), dma((H,)),
             dma, dma,
-            dma, dma((S,)),
-            dma, dma,
-            dma, dma,
-            dma, dma,
-            dma((4,)), dma((4,)),
+            dma, dma,
+            dma, dma,
+            dma, dma,
+            dma, dma,
+            dma((3,)), dma((3,)),
+            dma((max(1, third * S // SB),)), dma((max(1, third * S // SB),)),
             dma, dma,
             dma, dma,
             dma, dma,
             dma, dma,
             dma, dma,
             dma,
-            dma((5,)), dma((5,)),
+            dma((6,)), dma((6,)),
             dma,
         ],
         compiler_params=pltpu.CompilerParams(
             collective_id=0, has_side_effects=True, vmem_limit_bytes=LIMIT
         ),
         name="step",
-    )(guidance, rate, img, tx, rt, noise, old, reward)
+    )(guidance, rate, reward, img, tx, rt, noise, old)
 
 
 def on_device(S, NI, img_qkv, txt_kv, readout, old_velocity, noise, step_ratio, rewards, guidance):
@@ -775,13 +845,12 @@
     text = txt_kv[0, 0]
     tx = jnp.concatenate([text[:, 0], text[:, 1]], axis=0)
     scalar = lambda x: x.reshape(1, 1)
-    reward = jnp.broadcast_to(scalar(rewards), (8, D))
     grad, tgrad, rg, ratio = step_call(
-        S, NI, scalar(guidance), scalar(step_ratio), img, tx, readout.T, noise[0].T, old_velocity[0].T, reward
+        S, NI, scalar(guidance), scalar(step_ratio), scalar(rewards), img, tx, readout.T, noise[0].T, old_velocity[0].T
     )
     img_grad = grad.transpose(1, 0, 2)[None, None]
     txt_grad = jnp.stack([tgrad[:TXT], tgrad[TXT:]], axis=1)[None, None]
-    return (img_grad, txt_grad, rg.reshape(C, -1).T, ratio[0, :1])
+    return (img_grad, txt_grad, rg.reshape(C, -1).T, ratio.reshape(1))
 
 
 def solution(mesh):

time: 159 us -> 147 us (0.925); the launches traced: 156 us -> 147 us
  Pallas kernels: 145 us -> 136 us
  between operations: 2.59 us -> 4.4 us
  local copies, waits for them, and re-layouts: 7.72 us -> 5.93 us
    pallas_call x1, Pallas kernels: 145 us -> 136 us  [step_call(): pl.pallas_call(functools.partial(step_kernel, S, NI), out_shape=(jax.Shap...]
where the time goes in v3:
time: 147 us
  Pallas kernels  136 us (93%)
  local copies, waits for them, and re-layouts  5.93 us (4%)
  between operations  4.4 us (3%)
    pallas_call x1, Pallas kernels, step_call(): pl.pallas_call(functools.partial(step_kernel, S, NI), out_shape=(jax.Shap...  136 us
    unnamed x6, local copies, waits for them, and re-layouts  5.14 us

profile of v3, /device:TPU:5, one launch (start us, length us, event | category | flops | bytes accessed | tf_op | source)
XLA Modules:
  0.0 147.0 jit_solution(13369580428645548862)
XLA Ops:
  2.6 0.9 copy.15
  3.4 0.6 pad_maximum_fusion.tx
  4.1 136.0 %step.1 = (bf16[3,128,2048]{2,1,0:T(8,128)(2,1)}, bf16[16,2048]{1,0:T(8,128)(2,1)}, f32[4,16,2048]{2,1,0:T(8,128)}, f32[1,1]{1,0:T(1,128)}) custom-call(f32[1,1]{1,0:T(1,128)} %bitcast.35.guidance, f32[1,1]{1,0:T(1,128)} %bitcast.33.rate, f32[1,1]{1,0:T(1,128)} %bitcast.34.reward, bf16[3,128,2048]{2,1,0:T(8,128)(2,1)} %bitcast.37, ...), custom_call_target="tpu_custom_call" | custom-call | tf_op jit(solution)/shard_map/step/pallas_call | solution.py:744
  140.1 0.8 slice_bitcast_fusion.3
  140.9 0.7 copy.13
  141.6 0.0 copy-start
  141.6 2.8 %copy.22 = bf16[1,1,128,3,2048]{4,2,3,1,0:T(8,128)(2,1)} copy(bf16[1,1,128,3,2048]{4,2,3,1,0:T(8,128)(2,1)} %bitcast.36) | data formatting | bytes 3145728
  144.4 0.0 copy-done
  144.4 0.8 copy.23
  (2 shorter events, 0.0 us)
Async XLA Ops:
  141.6 2.8 %copy-start = (f32[4,16,2048]{2,1,0:T(8,128)S(1)}, f32[4,16,2048]{2,1,0:T(8,128)}, u32[]{:S(2)}) copy-start(f32[4,16,2048]{2,1,0:T(8,128)} %get-tuple-element.10) | copy-start | bytes 1572868

commit v4 on v3

--- a/solution.py
+++ b/solution.py
@@ -102,11 +102,11 @@
 
 
 def step_kernel(
-    S, NI, guidance, rate, reward, img, tx, rt, noise, old,
+    S, NI, guidance, rate, reward, img, txt, rt, noise, old,
     grad, tgrad, rg, ratio,
-    vbuf, vrp, txb, kv, text, qbuf, keys, keys_t, narrow, narrow_t, scores_a, scores_b, hold_0, hold_1, hold_2, hold_3, hold_text, weights, out_t, linv,
-    msg, got, g_own, g_all, part, parts, pair, rewards, reward_own, gl, gl_cols, delta, gk,
-    uo, xu, uown, uf, uto, xut, utf, ko, xk, kf, kto, xkt, ktf, dqb, ub, utb, ktb, dv, rgp, rx, rh, rhb, r1, a1, r2, a2, r3, a3, r4,
+    tx, vbuf, vrp, txb, kv, text, qbuf, keys, keys_t, narrow, narrow_t, scores_a, scores_b, hold_0, hold_1, hold_2, hold_3, hold_text, weights, out_t, linv,
+    msg, got, g_own, g_all, part, parts, pair, rewards, reward_own, gl, gl_cols, delta, gk, factor, held,
+    uo, xu, uown, uf, uto, xut, utf, ko, xk, kf, kto, xkt, ktf, dqb, ub, utb, ktb, dv, dkt, dvt, rgp, rx, rh, rhb, r1, a1, r2, a2, r3, a3, r4,
     vsem, ks, kr, qs, qr, ts, tr, fs, fr, fts, ftr, ms, mr, gs, gr, ps, pr, pairs, pairr, rs, rr,
     xs, xr, xus, xur, us, ur, uts, utr, dqs, dqr, dks, dkr, kts, ktr, dvsem, as_, ar, ls,
 ):
@@ -133,6 +133,8 @@
             pl.semaphore_signal(
                 barrier, inc=1, device_id={"cfg": core, "img": wrap(i + k, NI)}, device_id_type=MESH
             )
+    words = txt[...].astype(F32)
+    tx[...] = jnp.concatenate([words[:, 0], words[:, 1]], axis=0).astype(BF16)
     vcopy.wait()
     reward_own[...] = jnp.full(reward_own.shape, reward[0, 0], F32)
 
@@ -361,7 +363,7 @@
     def share(k, carry):
         zt = at_distance(k, 1)
         for yy in range(YN):
-            put(g_own, g_all.at[s], gs, gr, c, zt * YN + yy)
+            put(g_own, g_all.at[s], gs, gr.at[s], c, zt * YN + yy)
         return carry
 
     lax.fori_loop(0, ZN, share, 0)
@@ -375,9 +377,14 @@
     lax.fori_loop(0, S, tell, 0)
     gk[...] = jnp.zeros_like(gk)
 
-    drain(g_all, gr)
-
-    def divide(zs, carry):
+    cols_home = pl.ds(pl.multiple_of(head * D, D), D)
+    mine = pl.ds(pl.multiple_of(HALF * c, HALF), HALF)
+    FIRST = min(3, ZN)
+
+    def divide(n):
+        zs = at_distance(n, -1)
+        for yy in range(YN):
+            drain(g_all.at[zs * YN + yy], gr.at[zs * YN + yy])
         g_t = jnp.concatenate(
             [
                 unpack_pair(g_all[zs * YN + 2 * m].astype(F32), g_all[zs * YN + 2 * m + 1].astype(F32))
@@ -392,33 +399,63 @@
         gl[zs] = jnp.concatenate([hi, lo], axis=0)
         delta[zs] = jnp.sum((hi32 + lo.astype(F32)) * out_t[zs], axis=0, keepdims=True)
         gl_cols[zs] = jnp.concatenate([hi32, hi32], axis=0).T.astype(BF16)
-        return carry
-
-    lax.fori_loop(0, ZN, divide, 0)
+
+    def key_grads(n):
+        zs = at_distance(n, -1)
+        block = qbuf[pl.ds(zs * YN, YN)].reshape(QB, D)
+        g_t = gl[zs]
+        shift = delta[zs]
+
+        def one(rows, dq_t):
+            gp = jnp.dot(narrow[rows], g_t, preferred_element_type=F32)
+            ds = (weights[zs, rows].astype(F32) * (gp - shift)).astype(BF16)
+            gk[rows] += jnp.dot(ds, block, preferred_element_type=F32)
+            return dq_t + jnp.dot(keys_t[:, rows], ds, preferred_element_type=F32)
+
+        return over_keys(one, jnp.zeros((D, QB), F32)).T
+
+    def send_query_grads(n, rows):
+        zs = at_distance(n, -1)
+        dqb[pl.ds(zs * YN, YN)] = (rows * (factor[...] * D ** (-0.5))).astype(BF16).reshape(YN, HALF, D)
+        for yy in range(YN):
+            t = zs * YN + yy
+            put(dqb.at[t], grad.at[0, mine, cols_home], dqs, dqr, branch, t)
+
+    def first_blocks(n, carry):
+        divide(n)
+        held[n] = key_grads(n)
+        return carry
+
+    lax.fori_loop(0, FIRST, first_blocks, 0)
+
+    def other_blocks(n, carry):
+        divide(n)
+        return carry
+
+    lax.fori_loop(FIRST, ZN, other_blocks, 0)
 
     drain(parts, pr)
     pair[0] = jnp.sum(parts[...], axis=0)
     swap = away(pair.at[0], pair.at[1], pairs, pairr, other)
     swap.start()
-    if NI > 1:
-        drain(rewards.at[pl.ds(0, NI - 1)], rr)
-    own_reward = reward_own[...]
-    rewards[i] = own_reward
-    mean = jnp.sum(rewards[...], axis=0) / NI
-    square = jnp.sum(rewards[...] * rewards[...], axis=0) / NI
-    deviates = jnp.sqrt(jnp.maximum(square - mean * mean, 0.0))
-    advantage = (own_reward - mean) / jnp.maximum(deviates, 1.0)
-    swap.wait()
-    ratio_now = jnp.exp((pair[0] + pair[1]) / (2 * S * HALF * C))
-    clipped = jnp.clip(ratio_now, 0.8, 1.2)
-    keep = ratio_now * advantage <= clipped * advantage
-    gain = jnp.where(keep, -ratio_now * advantage, 0.0)
-    ratio[0, 0] = jnp.max(ratio_now)
-    f = (gain * (step * branch_share))[0:1, :]
-    fscale = f * D ** (-0.5)
-
-    cols_home = pl.ds(pl.multiple_of(head * D, D), D)
-    mine = pl.ds(pl.multiple_of(HALF * c, HALF), HALF)
+
+    def settle():
+        if NI > 1:
+            drain(rewards.at[pl.ds(0, NI - 1)], rr)
+        own_reward = reward_own[...]
+        rewards[i] = own_reward
+        mean = jnp.sum(rewards[...], axis=0) / NI
+        square = jnp.sum(rewards[...] * rewards[...], axis=0) / NI
+        deviates = jnp.sqrt(jnp.maximum(square - mean * mean, 0.0))
+        advantage = (own_reward - mean) / jnp.maximum(deviates, 1.0)
+        swap.wait()
+        ratio_now = jnp.exp((pair[0] + pair[1]) / (2 * S * HALF * C))
+        clipped = jnp.clip(ratio_now, 0.8, 1.2)
+        keep = ratio_now * advantage <= clipped * advantage
+        gain = jnp.where(keep, -ratio_now * advantage, 0.0)
+        ratio[0, 0] = jnp.max(ratio_now)
+        factor[...] = gain * (step * branch_share)
+
     NG = max(1, n3 // SB)
     GS = S // NG
     GR = third * GS
@@ -427,7 +464,7 @@
         total = jnp.dot(weights[0, rows], gl_cols[0], preferred_element_type=F32)
         for zs in range(1, ZN):
             total = total + jnp.dot(weights[zs, rows], gl_cols[zs], preferred_element_type=F32)
-        return total * f
+        return total
 
     def paired(p, r):
         a, b = (
@@ -442,7 +479,7 @@
     def send_u(r):
         swap_u(r).wait_recv()
         srcs = pl.ds(r * GS, GS)
-        uf[srcs] = (uown[srcs] + xu[srcs].astype(F32)).astype(BF16)
+        uf[srcs] = ((uown[srcs] + xu[srcs].astype(F32)) * factor[...]).astype(BF16)
 
         def one(k, carry):
             t = r * GS + k
@@ -472,6 +509,8 @@
         swap_u(r).start()
         uown[srcs] = paired(0, r)
 
+        pl.when(k == min(1, NG - 1))(settle)
+
         @pl.when(k > 0)
         def _():
             send_u(group(k - 1))
@@ -480,7 +519,9 @@
 
     lax.fori_loop(0, NG, narrow_group, 0)
     swaps[0].wait_recv()
-    utf[...] = (jnp.concatenate([no_keys, both_texts[0]], axis=1) + xut[...].astype(F32)).astype(BF16)
+    utf[...] = (
+        (jnp.concatenate([no_keys, both_texts[0]], axis=1) + xut[...].astype(F32)) * factor[...]
+    ).astype(BF16)
 
     def send_text(k, carry):
         put(utf.at[k], utb.at[head], uts, utr, branch, c * H + k)
@@ -488,6 +529,12 @@
 
     lax.fori_loop(0, H, send_text, 0)
     send_u(group(NG - 1))
+
+    def send_held(n, carry):
+        send_query_grads(n, held[n])
+        return carry
+
+    lax.fori_loop(0, FIRST, send_held, 0)
 
     def widen_all():
         drain(ub, ur)
@@ -511,7 +558,7 @@
             )
             wide = jnp.dot(spaced.astype(BF16), twice, preferred_element_type=F32)
             dv[:, at] = wide[: 2 * HALF].astype(BF16)
-            tgrad[:, at] = wide[2 * HALF :].astype(BF16)
+            dvt[:, at] = wide[2 * HALF + TXT :]
             values = jnp.concatenate([vbuf[:, at], tx[:, at]], axis=0)
             res = jnp.dot(spaced.T.astype(BF16), values, preferred_element_type=F32)
             rgp[:, at] = res[:C] + res[C:]
@@ -579,41 +626,29 @@
 
     steps = dict(
         widen_all=widen_all, readout_1=readout_1, readout_2=readout_2, readout_3=readout_3,
-        readout_4=readout_4, readout_5=readout_5, readout_6=readout_6,
+        readout_4=readout_4,
     )
 
-    def key_grads(n, carry):
-        zs = at_distance(n, -1)
-        block = qbuf[pl.ds(zs * YN, YN)].reshape(QB, D)
-        g_t = gl[zs]
-        shift = delta[zs]
-
-        def one(rows, dq_t):
-            gp = jnp.dot(narrow[rows], g_t, preferred_element_type=F32)
-            ds = (weights[zs, rows].astype(F32) * (gp - shift)).astype(BF16)
-            gk[rows] += jnp.dot(ds, block, preferred_element_type=F32)
-            return dq_t + jnp.dot(keys_t[:, rows], ds, preferred_element_type=F32)
-
-        dq_t = over_keys(one, jnp.zeros((D, QB), F32))
-        dqb[pl.ds(zs * YN, YN)] = (dq_t.T * fscale).astype(BF16).reshape(YN, HALF, D)
-        for yy in range(YN):
-            t = zs * YN + yy
-            put(dqb.at[t], grad.at[0, mine, cols_home], dqs, dqr, branch, t)
+    def other_key_grads(n, carry):
+        send_query_grads(n, key_grads(n))
         for at, what in EVENTS:
             pl.when(n == min(at, ZN - 1))(steps[what])
         return carry
 
-    lax.fori_loop(0, ZN, key_grads, 0)
+    lax.fori_loop(FIRST, ZN, other_key_grads, 0)
+    if ZN <= FIRST:
+        for at, what in EVENTS:
+            steps[what]()
 
     def image_keys(p):
         base = 2 * p * n3
         a = gk[base : base + n3].reshape(S, third, D)
         b = gk[base + n3 : base + 2 * n3].reshape(S, third, D)
-        return jnp.concatenate([a, b], axis=1) * fscale
+        return jnp.concatenate([a, b], axis=1) * (factor[...] * D ** (-0.5))
 
     def text_keys(p):
         k = gk[NKI + p * H * TXT : NKI + (p + 1) * H * TXT]
-        k = (k * fscale).reshape(H, TXT, D)
+        k = (k * (factor[...] * D ** (-0.5))).reshape(H, TXT, D)
         return jnp.concatenate([k, jnp.zeros_like(k)], axis=1)
 
     ko[...] = image_keys(1).astype(BF16)
@@ -624,13 +659,15 @@
     kf[...] = (image_keys(0) + xk[...].astype(F32)).astype(BF16)
 
     def send_key_grads(k, carry):
-        zt = at_distance(k, 1)
+        zt = at_distance(ZN - 1 - k, 1)
         for yy in range(YN):
             t = zt * YN + yy
             put(kf.at[t], grad.at[1, mine, cols_home], dks, dkr, branch, t)
         return carry
 
-    lax.fori_loop(0, ZN, send_key_grads, 0)
+    lax.fori_loop(0, ZN // 2, send_key_grads, 0)
+    readout_5()
+    lax.fori_loop(ZN // 2, ZN, send_key_grads, 0)
     swaps[2].wait_recv()
     ktf[...] = (text_keys(0) + xkt[...].astype(F32)).astype(BF16)
 
@@ -639,7 +676,6 @@
         return carry
 
     lax.fori_loop(0, H, send_text_keys, 0)
-
     readout_6()
 
     def sent(k, carry):
@@ -713,45 +749,45 @@
 
     def text_home(h, carry):
         at = pl.ds(pl.multiple_of(h * D, D), D)
-        t = ktb[h].astype(F32)
-        tgrad[:, at] = jnp.where(iota(t.shape, 0) < TXT, t, tgrad[:, at].astype(F32)).astype(BF16)
+        dkt[:, at] = ktb[h].astype(F32)[:TXT]
         return carry
 
     lax.fori_loop(0, H, text_home, 0)
+    tgrad[...] = jnp.stack([dkt[...], dvt[...]], axis=1).astype(BF16)
     drain(grad.at[0], dqr)
     drain(grad.at[1], dkr)
 
 
 EVENTS = (
-    (1, "widen_all"),
-    (1, "readout_1"),
-    (2, "readout_2"),
-    (4, "readout_3"),
-    (5, "readout_4"),
-    (7, "readout_5"),
+    (4, "widen_all"),
+    (4, "readout_1"),
+    (5, "readout_2"),
+    (6, "readout_3"),
+    (7, "readout_4"),
 )
 
 
-def step_call(S, NI, guidance, rate, reward, img, tx, rt, noise, old):
+def step_call(S, NI, guidance, rate, reward, img, txt, rt, noise, old):
     H, ZN, NP = S // 2, S // YN, 2 * NI
     HD = rt.shape[1]
     W, RY, third = HD // NP, C // YN, HALF // 2
     NK = (2 * HALF + TXT) * S
     dma = pltpu.SemaphoreType.DMA
-    tile = (8, D)
+    tile = (1, D)
     b = lambda *shape: pltpu.VMEM(shape, BF16)
     w = lambda *shape: pltpu.VMEM(shape, F32)
     return pl.pallas_call(
         functools.partial(step_kernel, S, NI),
         out_shape=(
             jax.ShapeDtypeStruct(img.shape, BF16),
-            jax.ShapeDtypeStruct((2 * TXT, HD), BF16),
+            jax.ShapeDtypeStruct((TXT, 2, HD), BF16),
             jax.ShapeDtypeStruct((YN, RY, HD), F32),
             jax.ShapeDtypeStruct((1, 1), F32),
         ),
         in_specs=[SMEM, SMEM, SMEM, ANY, VMEM, VMEM, VMEM, VMEM],
         out_specs=(ANY, VMEM, ANY, SMEM),
         scratch_shapes=[
+            b(2 * TXT, HD),
             b(*img.shape[1:]),
             b(H, 2, third, D),
             b(H, 2 * TXT, D),
@@ -782,6 +818,8 @@
             b(ZN, QB, D),
             w(ZN, 1, QB),
             w(NK, D),
+            w(*tile),
+            w(min(3, ZN), QB, D),
             b(S, third, D),
             b(S, third, D),
             w(S, third, D),
@@ -800,6 +838,8 @@
             b(H, 2 * TXT, D),
             b(H, 2 * TXT, D),
             b(*img.shape[1:]),
+            w(TXT, HD),
+            w(TXT, HD),
             w(C, HD),
             w(C, NI * W),
             w(C, NI * W),
@@ -818,7 +858,7 @@
             dma((S,)), dma((S,)),
             dma((H,)), dma((H,)),
             dma, dma,
-            dma, dma,
+            dma, dma((S,)),
             dma, dma,
             dma, dma,
             dma, dma,
@@ -837,20 +877,18 @@
             collective_id=0, has_side_effects=True, vmem_limit_bytes=LIMIT
         ),
         name="step",
-    )(guidance, rate, reward, img, tx, rt, noise, old)
+    )(guidance, rate, reward, img, txt, rt, noise, old)
 
 
 def on_device(S, NI, img_qkv, txt_kv, readout, old_velocity, noise, step_ratio, rewards, guidance):
     img = img_qkv[0, 0].transpose(1, 0, 2)
     text = txt_kv[0, 0]
-    tx = jnp.concatenate([text[:, 0], text[:, 1]], axis=0)
     scalar = lambda x: x.reshape(1, 1)
     grad, tgrad, rg, ratio = step_call(
-        S, NI, scalar(guidance), scalar(step_ratio), scalar(rewards), img, tx, readout.T, noise[0].T, old_velocity[0].T
+        S, NI, scalar(guidance), scalar(step_ratio), scalar(rewards), img, text, readout.T, noise[0].T, old_velocity[0].T
     )
     img_grad = grad.transpose(1, 0, 2)[None, None]
-    txt_grad = jnp.stack([tgrad[:TXT], tgrad[TXT:]], axis=1)[None, None]
-    return (img_grad, txt_grad, rg.reshape(C, -1).T, ratio.reshape(1))
+    return (img_grad, tgrad[None, None], rg.reshape(C, -1).T, ratio.reshape(1))
 
 
 def solution(mesh):

time: 147 us -> 140 us (0.952)
  Pallas kernels: 136 us -> 131 us
  local copies, waits for them, and re-layouts: 5.93 us -> 4.22 us
    pallas_call x1, Pallas kernels: 136 us -> 131 us  [step_call(): pl.pallas_call(functools.partial(step_kernel, S, NI), out_shape=(jax.Shap...]
    unnamed x6 -> x7, local copies, waits for them, and re-layouts: 5.14 us -> 4.22 us
where the time goes in v4:
time: 140 us; the launch traced here: 139 us
  Pallas kernels  131 us (94%)
  between operations  4.4 us (3%)
  local copies, waits for them, and re-layouts  4.22 us (3%)
    pallas_call x1, Pallas kernels, step_call(): pl.pallas_call(functools.partial(step_kernel, S, NI), out_shape=(jax.Shap...  131 us
    unnamed x7, local copies, waits for them, and re-layouts  4.22 us

profile of v4, /device:TPU:5, one launch (start us, length us, event | category | flops | bytes accessed | tf_op | source)
XLA Modules:
  0.0 139.3 jit_solution(11220304334099616533)
XLA Ops:
  2.6 130.7 %step.1 = (bf16[3,128,2048]{2,1,0:T(8,128)(2,1)}, bf16[8,2,2048]{2,1,0:T(2,128)(2,1)}, f32[4,16,2048]{2,1,0:T(8,128)}, f32[1,1]{1,0:T(1,128)}) custom-call(f32[1,1]{1,0:T(1,128)} %bitcast.24.guidance, f32[1,1]{1,0:T(1,128)} %bitcast.22.rate, f32[1,1]{1,0:T(1,128)} %bitcast.23.reward, bf16[3,128,2048]{2,1,0:T(8,128)(2,1)} %bitcast.26, ...), custom_call_target="tpu_custom_call" | custom-call | tf_op jit(solution)/shard_map/step/pallas_call | solution.py:779
  133.3 0.0 copy-start.1
  133.3 0.0 copy-start
  133.3 2.8 %copy.19 = bf16[1,1,128,3,2048]{4,2,3,1,0:T(8,128)(2,1)} copy(bf16[1,1,128,3,2048]{4,2,3,1,0:T(8,128)(2,1)} %bitcast.25) | data formatting | bytes 3145728
  136.1 0.0 copy-done.1
  136.1 0.6 copy.20
  136.7 0.0 copy-done
  136.7 0.8 copy.21
Async XLA Ops:
  133.3 2.8 %copy-start.1 = (bf16[8,2,2048]{2,1,0:T(2,128)(2,1)S(1)}, bf16[8,2,2048]{2,1,0:T(2,128)(2,1)}, u32[]{:S(2)}) copy-start(bf16[8,2,2048]{2,1,0:T(2,128)(2,1)} %get-tuple-element.9) | copy-start | bytes 196612
  133.3 3.4 %copy-start = (f32[4,16,2048]{2,1,0:T(8,128)S(1)}, f32[4,16,2048]{2,1,0:T(8,128)}, u32[]{:S(2)}) copy-start(f32[4,16,2048]{2,1,0:T(8,128)} %get-tuple-element.10) | copy-start | bytes 1572868

commit v5 on v4

--- a/solution.py
+++ b/solution.py
@@ -13,8 +13,10 @@
 TXT = 8
 YN = 4
 QB = 256
-KB = 1024
+KB = 4096
 SB = 256
+BB = 2176
+UB = 512
 ONES = 16
 MESH = pl.DeviceIdType.MESH
 F32 = jnp.float32
@@ -104,9 +106,9 @@
 def step_kernel(
     S, NI, guidance, rate, reward, img, txt, rt, noise, old,
     grad, tgrad, rg, ratio,
-    tx, vbuf, vrp, txb, kv, text, qbuf, keys, keys_t, narrow, narrow_t, scores_a, scores_b, hold_0, hold_1, hold_2, hold_3, hold_text, weights, out_t, linv,
+    tx, vbuf, vrp, txb, kv, text, qbuf, keys, keys_t, narrow, narrow_t, scores_a, scores_b, hold, hold_text, weights, out_t, linv,
     msg, got, g_own, g_all, part, parts, pair, rewards, reward_own, gl, gl_cols, delta, gk, factor, held,
-    uo, xu, uown, uf, uto, xut, utf, ko, xk, kf, kto, xkt, ktf, dqb, ub, utb, ktb, dv, dkt, dvt, rgp, rx, rh, rhb, r1, a1, r2, a2, r3, a3, r4,
+    uo, xu, uown, uf, uto, xut, utf, ko, xk, kf, kto, xkt, ktf, dqb, ub, utb, ktb, dv, dkt, dvt, rgp, rgb, r1, a1, r2, a2, r3, a3, r4, r4b,
     vsem, ks, kr, qs, qr, ts, tr, fs, fr, fts, ftr, ms, mr, gs, gr, ps, pr, pairs, pairr, rs, rr,
     xs, xr, xus, xur, us, ur, uts, utr, dqs, dqr, dks, dkr, kts, ktr, dvsem, as_, ar, ls,
 ):
@@ -117,7 +119,8 @@
     RY = C // YN
     NK = keys.shape[0]
     NKI = 2 * HALF * S
-    holds = (hold_0, hold_1, hold_2, hold_3)[: min(KB, NKI) // SB]
+    KT = min(KB, NKI)
+    subs = KT // SB
     third = HALF // 2
     n3 = third * S
     c, i, s = lax.axis_index("cfg"), lax.axis_index("img"), lax.axis_index("seq")
@@ -179,7 +182,7 @@
         return at_distance(jnp.where(n == 0, 0, jnp.where(n <= ZN - 3, n + 2, n - (ZN - 3))), sign)
 
     def send_keys(k, carry):
-        zt = at_distance(k // 2, 1)
+        zt = at_distance(ZN - 1 - k // 2, 1)
         h = 2 * zt + lax.rem(k, 2)
         chip = 2 * h + c
         cols = pl.ds(pl.multiple_of(h * D, D), D)
@@ -221,7 +224,7 @@
             narrow[rows] = jnp.concatenate([one, one], axis=0).T.astype(BF16)
 
     def arrive(n, carry):
-        zs = at_distance(n, -1)
+        zs = at_distance(ZN - 1 - n, -1)
         for yy in range(YN):
             src = zs * YN + yy
             drain(kv.at[0, src], kr.at[src])
@@ -239,7 +242,7 @@
     lax.fori_loop(0, H, arrive_text, 0)
 
     def arrive_other(n, carry):
-        zs = at_distance(n, -1)
+        zs = at_distance(ZN - 1 - n, -1)
         for yy in range(YN):
             drain(kv.at[1, zs * YN + yy], fr.at[zs * YN + yy])
         lay_out(1, zs)
@@ -264,8 +267,8 @@
     narrow[last] = jnp.concatenate([tvt, tvt], axis=0).T.astype(BF16)
 
     def over_keys(body, carry):
-        for at in range(0, NK, SB):
-            carry = body(slice(at, min(at + SB, NK)), carry)
+        for at in range(0, NK, BB):
+            carry = body(slice(at, min(at + BB, NK)), carry)
         return carry
 
     def queries_t(zs):
@@ -291,11 +294,10 @@
     low_top = jnp.full((8, QB), -jnp.inf, F32)
     no_mix = jnp.zeros((C + ONES, QB), F32)
     branch_share = jnp.where(branch == 0, guidance[0, 0], 1.0 - guidance[0, 0])
-    parts_of = NKI // KB
-    subs = KB // SB
+    parts_of = NKI // KT
 
     def chunk(k, sub):
-        return pl.ds(pl.multiple_of(k * KB + sub * SB, SB), SB)
+        return pl.ds(pl.multiple_of(k * KT + sub * SB, SB), SB)
 
     def first_scores(q_t):
         def body(k, t):
@@ -312,20 +314,20 @@
         next8 = score(then, last, q_t, low_top) if ahead else low_top
         weigh(now, zs, last, top, hold_text)
         mixed = mix(last, hold_text, no_mix)
-        holds[subs - 1][...] = jnp.zeros((SB, QB), BF16)
+        hold[subs - 1] = jnp.zeros((SB, QB), BF16)
 
         def body(k, carry):
             next8, mixed = carry
             for sub in range(subs):
                 before = chunk(jnp.maximum(k - 1, 0), subs - 1) if sub == 0 else chunk(k, sub - 1)
-                mixed = mix(before, holds[sub - 1], mixed)
+                mixed = mix(before, hold.at[(sub - 1) % subs], mixed)
                 if ahead:
                     next8 = score(then, chunk(k, sub), q_t, next8)
-                weigh(now, zs, chunk(k, sub), top, holds[sub])
+                weigh(now, zs, chunk(k, sub), top, hold.at[sub])
             return next8, mixed
 
         next8, mixed = lax.fori_loop(0, parts_of, body, (next8, mixed))
-        mixed = mix(chunk(parts_of - 1, subs - 1), holds[subs - 1], mixed)
+        mixed = mix(chunk(parts_of - 1, subs - 1), hold.at[subs - 1], mixed)
         inverse = 1.0 / mixed[C : C + 1]
         linv[zs] = inverse
         normal = mixed[:C] * inverse
@@ -456,7 +458,7 @@
         ratio[0, 0] = jnp.max(ratio_now)
         factor[...] = gain * (step * branch_share)
 
-    NG = max(1, n3 // SB)
+    NG = max(1, n3 // UB)
     GS = S // NG
     GR = third * GS
 
@@ -507,13 +509,13 @@
         srcs = pl.ds(r * GS, GS)
         uo[srcs] = paired(1, r).astype(BF16)
         swap_u(r).start()
-        uown[srcs] = paired(0, r)
-
         pl.when(k == min(1, NG - 1))(settle)
 
         @pl.when(k > 0)
         def _():
             send_u(group(k - 1))
+
+        uown[srcs] = paired(0, r)
 
         return carry
 
@@ -566,10 +568,7 @@
         some(H, widen)
         pltpu.make_async_copy(dv, grad.at[2], dvsem).start()
 
-    HW = NI * W
-
-    def half(core):
-        return pl.ds(pl.multiple_of(core * HW, D), HW)
+    me = 2 * i + c
 
     def piece(n):
         return pl.ds(pl.multiple_of(n * W, D), W)
@@ -577,22 +576,21 @@
     def strip(n):
         return pl.ds(pl.multiple_of(n * RY, 8), RY)
 
+    def peers():
+        for k in range(NI):
+            n = wrap(i + k, NI)
+            for core in (c, 1 - c) if k else (1 - c,):
+                yield 2 * n + core, {"cfg": core, "img": n}
+
     def readout_1():
-        away(rgp.at[:, half(1 - c)], rx, as_.at[0], ar.at[0], other).start()
-
-    def readout_2():
-        drain(rx, ar.at[0])
-        rh[...] = rgp[:, half(c)] + rx[...]
-        rhb[...] = rh[...].astype(BF16)
-        for k in range(1, NI):
-            n = wrap(i + k, NI)
-            away(rhb.at[:, piece(n)], r1.at[i], as_.at[5], ar.at[5], {"img": n}).start()
+        rgb[...] = rgp[...].astype(BF16)
+        for n, device in peers():
+            away(rgb.at[:, piece(n)], r1.at[me], as_.at[0], ar.at[0], device).start()
 
     def readout_3():
-        if NI > 1:
-            drain(r1.at[pl.ds(0, NI - 1)], ar.at[5])
-        r1[i] = jnp.zeros((C, W), BF16)
-        a1[...] = jnp.sum(r1[...].astype(F32), axis=0) + rh[:, piece(i)]
+        drain(r1.at[pl.ds(0, NP - 1)], ar.at[0])
+        r1[me] = jnp.zeros((C, W), BF16)
+        a1[...] = jnp.sum(r1[...].astype(F32), axis=0) + rgp[:, piece(me)]
         for k in range(1, YN):
             n = wrap(y + k, YN)
             away(a1.at[strip(n)], r2.at[y], as_.at[1], ar.at[1], {"seq": z * YN + n}).start()
@@ -617,28 +615,17 @@
     def readout_6():
         drain(r4.at[pl.ds(0, YN - 1)], ar.at[3])
         r4[y] = a3[...]
-        to = rg.at[:, :, pl.ds(pl.multiple_of(c * HW + i * W, D), W)]
-        pltpu.make_async_copy(r4, to, ls).start()
-        for k in range(NI):
-            n = wrap(i + k, NI)
-            for core in (c, 1 - c) if k else (1 - c,):
-                away(r4, to, as_.at[4], ar.at[4], {"cfg": core, "img": n}).start()
-
-    steps = dict(
-        widen_all=widen_all, readout_1=readout_1, readout_2=readout_2, readout_3=readout_3,
-        readout_4=readout_4,
-    )
+        r4b[...] = r4[...].astype(BF16)
+        to = rg.at[:, :, piece(me)]
+        pltpu.make_async_copy(r4b, to, ls).start()
+        for _, device in peers():
+            away(r4b, to, as_.at[4], ar.at[4], device).start()
 
     def other_key_grads(n, carry):
         send_query_grads(n, key_grads(n))
-        for at, what in EVENTS:
-            pl.when(n == min(at, ZN - 1))(steps[what])
         return carry
 
     lax.fori_loop(FIRST, ZN, other_key_grads, 0)
-    if ZN <= FIRST:
-        for at, what in EVENTS:
-            steps[what]()
 
     def image_keys(p):
         base = 2 * p * n3
@@ -655,6 +642,8 @@
     swaps[1].start()
     kto[...] = text_keys(1).astype(BF16)
     swaps[2].start()
+    widen_all()
+    readout_1()
     swaps[1].wait_recv()
     kf[...] = (image_keys(0) + xk[...].astype(F32)).astype(BF16)
 
@@ -665,9 +654,10 @@
             put(kf.at[t], grad.at[1, mine, cols_home], dks, dkr, branch, t)
         return carry
 
-    lax.fori_loop(0, ZN // 2, send_key_grads, 0)
-    readout_5()
-    lax.fori_loop(ZN // 2, ZN, send_key_grads, 0)
+    lax.fori_loop(0, ZN // 4, send_key_grads, 0)
+    readout_3()
+    readout_4()
+    lax.fori_loop(ZN // 4, ZN, send_key_grads, 0)
     swaps[2].wait_recv()
     ktf[...] = (text_keys(0) + xkt[...].astype(F32)).astype(BF16)
 
@@ -676,6 +666,8 @@
         return carry
 
     lax.fori_loop(0, H, send_text_keys, 0)
+
+    readout_5()
     readout_6()
 
     def sent(k, carry):
@@ -704,16 +696,15 @@
         drain(rewards.at[pl.ds(0, NI - 1)], rs)
     for w in swaps:
         w.wait_send()
-    drain(rx, as_.at[0])
-    if NI > 1:
-        drain(r1.at[pl.ds(0, NI - 1)], as_.at[5])
+    drain(r1.at[pl.ds(0, NP - 1)], as_.at[0])
     drain(r2.at[pl.ds(0, YN - 1)], as_.at[1])
     if ZN > 1:
         drain(r3.at[pl.ds(0, ZN - 1)], as_.at[2])
     drain(r4.at[pl.ds(0, YN - 1)], as_.at[3])
-    drain(rgp.at[:, pl.ds(0, (NP - 1) * W)], as_.at[4])
-    drain(r4, ls)
-    drain(rgp.at[:, pl.ds(0, (NP - 1) * W)], ar.at[4])
+    rest = dv.at[pl.ds(0, C), pl.ds(0, (NP - 1) * W)]
+    drain(rest, as_.at[4])
+    drain(r4b, ls)
+    drain(rest, ar.at[4])
 
     def swapped_u(r, carry):
         swap_u(r).wait_send()
@@ -756,15 +747,6 @@
     tgrad[...] = jnp.stack([dkt[...], dvt[...]], axis=1).astype(BF16)
     drain(grad.at[0], dqr)
     drain(grad.at[1], dkr)
-
-
-EVENTS = (
-    (4, "widen_all"),
-    (4, "readout_1"),
-    (5, "readout_2"),
-    (6, "readout_3"),
-    (7, "readout_4"),
-)
 
 
 def step_call(S, NI, guidance, rate, reward, img, txt, rt, noise, old):
@@ -781,7 +763,7 @@
         out_shape=(
             jax.ShapeDtypeStruct(img.shape, BF16),
             jax.ShapeDtypeStruct((TXT, 2, HD), BF16),
-            jax.ShapeDtypeStruct((YN, RY, HD), F32),
+            jax.ShapeDtypeStruct((YN, RY, HD), BF16),
             jax.ShapeDtypeStruct((1, 1), F32),
         ),
         in_specs=[SMEM, SMEM, SMEM, ANY, VMEM, VMEM, VMEM, VMEM],
@@ -800,7 +782,7 @@
             b(C + ONES, NK),
             w(NK, QB),
             w(NK, QB),
-            *([b(SB, QB)] * 4),
+            b(KB // SB, SB, QB),
             b(TXT * S, QB),
             b(ZN, NK, QB),
             w(ZN, C, QB),
@@ -841,16 +823,15 @@
             w(TXT, HD),
             w(TXT, HD),
             w(C, HD),
-            w(C, NI * W),
-            w(C, NI * W),
-            b(C, NI * W),
-            b(NI, C, W),
+            b(C, HD),
+            b(NP, C, W),
             w(C, W),
             w(YN, RY, W),
             w(RY, W),
             w(ZN, RY, W),
             w(RY, W),
             w(YN, RY, W),
+            b(YN, RY, W),
             dma,
             dma((H, 2)), dma((S,)),
             dma((H, 2)), dma((S,)),
@@ -863,14 +844,14 @@
             dma, dma,
             dma, dma,
             dma((3,)), dma((3,)),
-            dma((max(1, third * S // SB),)), dma((max(1, third * S // SB),)),
+            dma((max(1, third * S // UB),)), dma((max(1, third * S // UB),)),
             dma, dma,
             dma, dma,
             dma, dma,
             dma, dma,
             dma, dma,
             dma,
-            dma((6,)), dma((6,)),
+            dma((5,)), dma((5,)),
             dma,
         ],
         compiler_params=pltpu.CompilerParams(
@@ -888,7 +869,7 @@
         S, NI, scalar(guidance), scalar(step_ratio), scalar(rewards), img, text, readout.T, noise[0].T, old_velocity[0].T
     )
     img_grad = grad.transpose(1, 0, 2)[None, None]
-    return (img_grad, tgrad[None, None], rg.reshape(C, -1).T, ratio.reshape(1))
+    return (img_grad, tgrad[None, None], rg.reshape(C, -1).T.astype(F32), ratio.reshape(1))
 
 
 def solution(mesh):

time: 140 us -> 126 us (0.900); the launches traced: 139 us -> 124 us
  Pallas kernels: 131 us -> 114 us
  other arithmetic: 0 us -> 1.78 us
    pallas_call x1, Pallas kernels: 131 us -> 114 us  [step_call(): pl.pallas_call(functools.partial(step_kernel, S, NI), out_shape=(jax.Shap...]
    convert_element_type x0 -> x1, other arithmetic: none -> 1.78 us  [on_device(): rg.reshape(C, -1).T.astype(F32)]
    unnamed x7 -> x4, local copies, waits for them, and re-layouts: 4.22 us -> 3.39 us
where the time goes in v5:
time: 126 us; the launch traced here: 124 us
  Pallas kernels  114 us (90%)
  between operations  4.32 us (3%)
  local copies, waits for them, and re-layouts  3.39 us (3%)
  other arithmetic  1.78 us (1%)
    pallas_call x1, Pallas kernels, step_call(): pl.pallas_call(functools.partial(step_kernel, S, NI), out_shape=(jax.Shap...  114 us
    unnamed x4, local copies, waits for them, and re-layouts  3.39 us

profile of v5, /device:TPU:5, one launch (start us, length us, event | category | flops | bytes accessed | tf_op | source)
XLA Modules:
  0.0 123.7 jit_solution(7935327170525299707)
XLA Ops:
  2.6 114.3 %step.1 = (bf16[3,128,2048]{2,1,0:T(8,128)(2,1)}, bf16[8,2,2048]{2,1,0:T(2,128)(2,1)}, bf16[4,16,2048]{2,1,0:T(8,128)(2,1)}, f32[1,1]{1,0:T(1,128)}) custom-call(f32[1,1]{1,0:T(1,128)} %bitcast.26.guidance, f32[1,1]{1,0:T(1,128)} %bitcast.24.rate, f32[1,1]{1,0:T(1,128)} %bitcast.25.reward, bf16[3,128,2048]{2,1,0:T(8,128)(2,1)} %bitcast.28, ...), custom_call_target="tpu_custom_call" | custom-call | tf_op jit(solution)/shard_map/step/pallas_call | solution.py:761
  116.8 1.8 %convert_bitcast_fusion = f32[2048,64]{0,1:T(8,128)} fusion(bf16[4,16,2048]{2,1,0:T(8,128)(2,1)} %get-tuple-element.10), kind=kLoop, calls=%fused_computation | loop fusion | flops 131072 | bytes 786432 | tf_op jit(solution)/shard_map/convert_element_type | solution.py:872
  118.6 0.0 copy-start
  118.6 2.8 %copy.18 = bf16[1,1,128,3,2048]{4,2,3,1,0:T(8,128)(2,1)} copy(bf16[1,1,128,3,2048]{4,2,3,1,0:T(8,128)(2,1)} %bitcast.27) | data formatting | bytes 3145728
  121.4 0.0 copy-done
  121.4 0.6 copy.19
Async XLA Ops:
  118.6 2.8 %copy-start = (bf16[8,2,2048]{2,1,0:T(2,128)(2,1)S(1)}, bf16[8,2,2048]{2,1,0:T(2,128)(2,1)}, u32[]{:S(2)}) copy-start(bf16[8,2,2048]{2,1,0:T(2,128)(2,1)} %get-tuple-element.9) | copy-start | bytes 196612

commit v6 on v5

--- a/solution.py
+++ b/solution.py
@@ -108,7 +108,7 @@
     grad, tgrad, rg, ratio,
     tx, vbuf, vrp, txb, kv, text, qbuf, keys, keys_t, narrow, narrow_t, scores_a, scores_b, hold, hold_text, weights, out_t, linv,
     msg, got, g_own, g_all, part, parts, pair, rewards, reward_own, gl, gl_cols, delta, gk, factor, held,
-    uo, xu, uown, uf, uto, xut, utf, ko, xk, kf, kto, xkt, ktf, dqb, ub, utb, ktb, dv, dkt, dvt, rgp, rgb, r1, a1, r2, a2, r3, a3, r4, r4b,
+    uo, xu, uown, uf, uto, xut, utf, ko, xk, kf, kto, xkt, ktf, dqb, ub, utb, ktb, dv, dkt, dvt, rgp, rgb, r1, a2, r3, a3,
     vsem, ks, kr, qs, qr, ts, tr, fs, fr, fts, ftr, ms, mr, gs, gr, ps, pr, pairs, pairr, rs, rr,
     xs, xr, xus, xur, us, ur, uts, utr, dqs, dqr, dks, dkr, kts, ktr, dvsem, as_, ar, ls,
 ):
@@ -133,9 +133,13 @@
     barrier = signal_plane(S)
     for k in range(1, NI):
         for core in range(2):
-            pl.semaphore_signal(
-                barrier, inc=1, device_id={"cfg": core, "img": wrap(i + k, NI)}, device_id_type=MESH
-            )
+            for yy in range(YN):
+                pl.semaphore_signal(
+                    barrier,
+                    inc=1,
+                    device_id={"cfg": core, "img": wrap(i + k, NI), "seq": z * YN + yy},
+                    device_id_type=MESH,
+                )
     words = txt[...].astype(F32)
     tx[...] = jnp.concatenate([words[:, 0], words[:, 1]], axis=0).astype(BF16)
     vcopy.wait()
@@ -167,7 +171,7 @@
         lax.fori_loop(0, count // at_once, trip, 0)
 
     some(H, squeeze)
-    pl.semaphore_wait(barrier, 2 * S - 1 + 2 * (NI - 1))
+    pl.semaphore_wait(barrier, 2 * S - 1 + 2 * (NI - 1) * YN)
 
     side = s // H
 
@@ -574,52 +578,38 @@
         return pl.ds(pl.multiple_of(n * W, D), W)
 
     def strip(n):
-        return pl.ds(pl.multiple_of(n * RY, 8), RY)
+        return pl.ds(pl.multiple_of(n * RY, RY), RY)
 
     def peers():
-        for k in range(NI):
-            n = wrap(i + k, NI)
-            for core in (c, 1 - c) if k else (1 - c,):
-                yield 2 * n + core, {"cfg": core, "img": n}
+        for k in range(YN):
+            yy = wrap(y + k, YN)
+            for kk in range(NI):
+                n = wrap(i + kk, NI)
+                for core in (c, 1 - c) if k + kk else (1 - c,):
+                    yield 2 * n + core, yy, {"cfg": core, "img": n, "seq": z * YN + yy}
 
     def readout_1():
         rgb[...] = rgp[...].astype(BF16)
-        for n, device in peers():
-            away(rgb.at[:, piece(n)], r1.at[me], as_.at[0], ar.at[0], device).start()
-
-    def readout_3():
-        drain(r1.at[pl.ds(0, NP - 1)], ar.at[0])
-        r1[me] = jnp.zeros((C, W), BF16)
-        a1[...] = jnp.sum(r1[...].astype(F32), axis=0) + rgp[:, piece(me)]
-        for k in range(1, YN):
-            n = wrap(y + k, YN)
-            away(a1.at[strip(n)], r2.at[y], as_.at[1], ar.at[1], {"seq": z * YN + n}).start()
-
-    def readout_4():
-        drain(r2.at[pl.ds(0, YN - 1)], ar.at[1])
-        r2[y] = a1[strip(y), :]
-        a2[...] = jnp.sum(r2[...], axis=0)
+        for n, yy, device in peers():
+            away(rgb.at[strip(yy), piece(n)], r1.at[y * NP + me], as_.at[0], ar.at[0], device).start()
+
+    def readout_2():
+        drain(r1.at[pl.ds(0, NP * YN - 1)], ar.at[0])
+        r1[y * NP + me] = rgb[strip(y), piece(me)]
+        a2[...] = jnp.sum(r1[...].astype(F32), axis=0).astype(BF16)
         for k in range(1, ZN):
             n = wrap(z + k, ZN)
-            away(a2, r3.at[z], as_.at[2], ar.at[2], {"seq": n * YN + y}).start()
-
-    def readout_5():
+            away(a2, r3.at[z], as_.at[1], ar.at[1], {"seq": n * YN + y}).start()
+
+    def readout_3():
         if ZN > 1:
-            drain(r3.at[pl.ds(0, ZN - 1)], ar.at[2])
+            drain(r3.at[pl.ds(0, ZN - 1)], ar.at[1])
         r3[z] = a2[...]
-        a3[...] = jnp.sum(r3[...], axis=0)
-        for k in range(1, YN):
-            n = wrap(y + k, YN)
-            away(a3, r4.at[y], as_.at[3], ar.at[3], {"seq": z * YN + n}).start()
-
-    def readout_6():
-        drain(r4.at[pl.ds(0, YN - 1)], ar.at[3])
-        r4[y] = a3[...]
-        r4b[...] = r4[...].astype(BF16)
-        to = rg.at[:, :, piece(me)]
-        pltpu.make_async_copy(r4b, to, ls).start()
-        for _, device in peers():
-            away(r4b, to, as_.at[4], ar.at[4], device).start()
+        a3[...] = jnp.sum(r3[...].astype(F32), axis=0).astype(BF16)
+        to = rg.at[y, :, piece(me)]
+        pltpu.make_async_copy(a3, to, ls).start()
+        for _, _, device in peers():
+            away(a3, to, as_.at[2], ar.at[2], device).start()
 
     def other_key_grads(n, carry):
         send_query_grads(n, key_grads(n))
@@ -654,10 +644,9 @@
             put(kf.at[t], grad.at[1, mine, cols_home], dks, dkr, branch, t)
         return carry
 
-    lax.fori_loop(0, ZN // 4, send_key_grads, 0)
-    readout_3()
-    readout_4()
-    lax.fori_loop(ZN // 4, ZN, send_key_grads, 0)
+    lax.fori_loop(0, ZN // 8, send_key_grads, 0)
+    readout_2()
+    lax.fori_loop(ZN // 8, ZN, send_key_grads, 0)
     swaps[2].wait_recv()
     ktf[...] = (text_keys(0) + xkt[...].astype(F32)).astype(BF16)
 
@@ -667,8 +656,7 @@
 
     lax.fori_loop(0, H, send_text_keys, 0)
 
-    readout_5()
-    readout_6()
+    readout_3()
 
     def sent(k, carry):
         chip = 2 * k + c
@@ -696,15 +684,13 @@
         drain(rewards.at[pl.ds(0, NI - 1)], rs)
     for w in swaps:
         w.wait_send()
-    drain(r1.at[pl.ds(0, NP - 1)], as_.at[0])
-    drain(r2.at[pl.ds(0, YN - 1)], as_.at[1])
+    rest = r1.at[pl.ds(0, NP * YN - 1)]
+    drain(rest, as_.at[0])
     if ZN > 1:
-        drain(r3.at[pl.ds(0, ZN - 1)], as_.at[2])
-    drain(r4.at[pl.ds(0, YN - 1)], as_.at[3])
-    rest = dv.at[pl.ds(0, C), pl.ds(0, (NP - 1) * W)]
-    drain(rest, as_.at[4])
-    drain(r4b, ls)
-    drain(rest, ar.at[4])
+        drain(r3.at[pl.ds(0, ZN - 1)], as_.at[1])
+    drain(rest, as_.at[2])
+    drain(a3, ls)
+    drain(rest, ar.at[2])
 
     def swapped_u(r, carry):
         swap_u(r).wait_send()
@@ -824,14 +810,10 @@
             w(TXT, HD),
             w(C, HD),
             b(C, HD),
-            b(NP, C, W),
-            w(C, W),
-            w(YN, RY, W),
-            w(RY, W),
-            w(ZN, RY, W),
-            w(RY, W),
-            w(YN, RY, W),
-            b(YN, RY, W),
+            b(NP * YN, RY, W),
+            b(RY, W),
+            b(ZN, RY, W),
+            b(RY, W),
             dma,
             dma((H, 2)), dma((S,)),
             dma((H, 2)), dma((S,)),
@@ -851,7 +833,7 @@
             dma, dma,
             dma, dma,
             dma,
-            dma((5,)), dma((5,)),
+            dma((3,)), dma((3,)),
             dma,
         ],
         compiler_params=pltpu.CompilerParams(

time: 126 us -> 123 us (0.976)
  Pallas kernels: 114 us -> 112 us
    pallas_call x1, Pallas kernels: 114 us -> 112 us  [step_call(): pl.pallas_call(functools.partial(step_kernel, S, NI), out_shape=(jax.Shap...]
where the time goes in v6:
time: 123 us; the launch traced here: 121 us
  Pallas kernels  112 us (91%)
  between operations  4.32 us (4%)
  local copies, waits for them, and re-layouts  3.39 us (3%)
  other arithmetic  1.78 us (1%)
    pallas_call x1, Pallas kernels, step_call(): pl.pallas_call(functools.partial(step_kernel, S, NI), out_shape=(jax.Shap...  112 us
    unnamed x4, local copies, waits for them, and re-layouts  3.39 us

profile of v6, /device:TPU:5, one launch (start us, length us, event | category | flops | bytes accessed | tf_op | source)
XLA Modules:
  0.0 121.1 jit_solution(2837537382111312978)
XLA Ops:
  2.6 111.6 %step.1 = (bf16[3,128,2048]{2,1,0:T(8,128)(2,1)}, bf16[8,2,2048]{2,1,0:T(2,128)(2,1)}, bf16[4,16,2048]{2,1,0:T(8,128)(2,1)}, f32[1,1]{1,0:T(1,128)}) custom-call(f32[1,1]{1,0:T(1,128)} %bitcast.26.guidance, f32[1,1]{1,0:T(1,128)} %bitcast.24.rate, f32[1,1]{1,0:T(1,128)} %bitcast.25.reward, bf16[3,128,2048]{2,1,0:T(8,128)(2,1)} %bitcast.28, ...), custom_call_target="tpu_custom_call" | custom-call | tf_op jit(solution)/shard_map/step/pallas_call | solution.py:747
  114.2 1.8 %convert_bitcast_fusion = f32[2048,64]{0,1:T(8,128)} fusion(bf16[4,16,2048]{2,1,0:T(8,128)(2,1)} %get-tuple-element.10), kind=kLoop, calls=%fused_computation | loop fusion | flops 131072 | bytes 786432 | tf_op jit(solution)/shard_map/convert_element_type | solution.py:854
  115.9 0.0 copy-start
  116.0 2.8 %copy.18 = bf16[1,1,128,3,2048]{4,2,3,1,0:T(8,128)(2,1)} copy(bf16[1,1,128,3,2048]{4,2,3,1,0:T(8,128)(2,1)} %bitcast.27) | data formatting | bytes 3145728
  118.7 0.0 copy-done
  118.7 0.6 copy.19
Async XLA Ops:
  115.9 2.8 %copy-start = (bf16[8,2,2048]{2,1,0:T(2,128)(2,1)S(1)}, bf16[8,2,2048]{2,1,0:T(2,128)(2,1)}, u32[]{:S(2)}) copy-start(bf16[8,2,2048]{2,1,0:T(2,128)(2,1)} %get-tuple-element.9) | copy-start | bytes 196612

commit v7 on v6

--- a/solution.py
+++ b/solution.py
@@ -628,12 +628,12 @@
         k = (k * (factor[...] * D ** (-0.5))).reshape(H, TXT, D)
         return jnp.concatenate([k, jnp.zeros_like(k)], axis=1)
 
+    widen_all()
+    readout_1()
     ko[...] = image_keys(1).astype(BF16)
     swaps[1].start()
     kto[...] = text_keys(1).astype(BF16)
     swaps[2].start()
-    widen_all()
-    readout_1()
     swaps[1].wait_recv()
     kf[...] = (image_keys(0) + xk[...].astype(F32)).astype(BF16)
 
@@ -644,9 +644,8 @@
             put(kf.at[t], grad.at[1, mine, cols_home], dks, dkr, branch, t)
         return carry
 
-    lax.fori_loop(0, ZN // 8, send_key_grads, 0)
     readout_2()
-    lax.fori_loop(ZN // 8, ZN, send_key_grads, 0)
+    lax.fori_loop(0, ZN, send_key_grads, 0)
     swaps[2].wait_recv()
     ktf[...] = (text_keys(0) + xkt[...].astype(F32)).astype(BF16)
 

time: 123 us -> 123 us (level)
  no operation moved by 1% of the time
where the time goes in v7:
time: 123 us; the launch traced here: 122 us
  Pallas kernels  112 us (91%)
  between operations  4.32 us (4%)
  local copies, waits for them, and re-layouts  3.39 us (3%)
  other arithmetic  1.78 us (1%)
    pallas_call x1, Pallas kernels, step_call(): pl.pallas_call(functools.partial(step_kernel, S, NI), out_shape=(jax.Shap...  112 us
    unnamed x4, local copies, waits for them, and re-layouts  3.39 us

profile of v7, /device:TPU:5, one launch (start us, length us, event | category | flops | bytes accessed | tf_op | source)
XLA Modules:
  0.0 121.5 jit_solution(5005295636500961079)
XLA Ops:
  2.6 112.0 %step.1 = (bf16[3,128,2048]{2,1,0:T(8,128)(2,1)}, bf16[8,2,2048]{2,1,0:T(2,128)(2,1)}, bf16[4,16,2048]{2,1,0:T(8,128)(2,1)}, f32[1,1]{1,0:T(1,128)}) custom-call(f32[1,1]{1,0:T(1,128)} %bitcast.26.guidance, f32[1,1]{1,0:T(1,128)} %bitcast.24.rate, f32[1,1]{1,0:T(1,128)} %bitcast.25.reward, bf16[3,128,2048]{2,1,0:T(8,128)(2,1)} %bitcast.28, ...), custom_call_target="tpu_custom_call" | custom-call | tf_op jit(solution)/shard_map/step/pallas_call | solution.py:746
  114.6 1.8 %convert_bitcast_fusion = f32[2048,64]{0,1:T(8,128)} fusion(bf16[4,16,2048]{2,1,0:T(8,128)(2,1)} %get-tuple-element.10), kind=kLoop, calls=%fused_computation | loop fusion | flops 131072 | bytes 786432 | tf_op jit(solution)/shard_map/convert_element_type | solution.py:853
  116.4 0.0 copy-start
  116.4 2.8 %copy.18 = bf16[1,1,128,3,2048]{4,2,3,1,0:T(8,128)(2,1)} copy(bf16[1,1,128,3,2048]{4,2,3,1,0:T(8,128)(2,1)} %bitcast.27) | data formatting | bytes 3145728
  119.2 0.0 copy-done
  119.2 0.6 copy.19
Async XLA Ops:
  116.4 2.8 %copy-start = (bf16[8,2,2048]{2,1,0:T(2,128)(2,1)S(1)}, bf16[8,2,2048]{2,1,0:T(2,128)(2,1)}, u32[]{:S(2)}) copy-start(bf16[8,2,2048]{2,1,0:T(2,128)(2,1)} %get-tuple-element.9) | copy-start | bytes 196612
